TPU v7x, 128 devices: a whole 4x4x4 slice. The times are simulated.
128 devices in a mesh: row: 8 (over x, z_hi), col: 16 (over y, z_lo, core).
Axes of the slice: x: 4, y: 4, z: 4 (z_hi: 2, z_lo: 2; z = z_hi * 2 + z_lo), core: 2. Of those that a mesh axis runs over, the one named last changes fastest.
Arguments:
- matrix: float32 [16384, 16384], P('row', 'col'), may hold values from -6 to 6
- factor_inverse: float32 [512, 512], replicated, may hold values from -0.25 to 0.25
- panel: int32 [1], replicated, may hold values from 0 to 31
- split_index: int32 [1], replicated, may hold values from 4096 to 12288
Outputs:
- halves: float32 [16384, 512], P('col')
All inputs are finite; a program needn't handle non-finite values.
Results may differ from a plain program's by a relative error of at most 0.000071.
Values sent between devices are 32-bit elements; how exact they have to be, the bound alone decides.
No kernel may reach another device: no remote copies, remote signals or barrier semaphores. Data moves between devices by JAX's collectives and lax.ppermute only.
A program may use at most 64 MiB of HBM per device.

v0:
```python
import functools

import jax
import jax.numpy as jnp
from jax import lax
from jax.experimental import pallas as pl
from jax.experimental.pallas import tpu as pltpu
from jax.sharding import Mesh, PartitionSpec as P


ROW = ("x", "zh")
GRID = ("y", "zl")
COL = ("y", "zl", "core")
ALL = ROW + COL
SIZES = (4, 2, 4, 2, 2)
F32, BF16 = jnp.float32, jnp.bfloat16
BLK = 128
REL = ((2, 1), (2, 0), (3, 0), (1, 1), (3, 1), (1, 0), (0, 1), (0, 0))


def split(v):
    hi = v.astype(BF16)
    return hi, (v - hi.astype(F32)).astype(BF16)


def three(ah, al, bh, bl, dims):
    def one(p, q):
        return lax.dot_general(p, q, (dims, ((), ())), preferred_element_type=F32)

    return one(ah, bh) + (one(ah, bl) + one(al, bh))


def join_split(refs, hi, lo):
    @pl.when(pl.program_id(0) == 0)
    def _():
        for k, ref in enumerate(refs):
            rows = pl.ds(k * BLK, BLK)
            hi[rows, :], lo[rows, :] = split(ref[...])


def gram_kernel(n, has_prev, me, *refs):
    m, c, rest = refs[:n], refs[n : 2 * n], refs[2 * n :]
    out, ch, cl = rest[has_prev:]
    join_split(c, ch, cl)
    mh, ml = split(jnp.concatenate([r[...] for r in m], 0))
    made = three(mh, ml, ch[...], cl[...], ((0,), (0,)))
    out[...] = made + rest[0][...] if has_prev else made


def group_spot(s, axis, d):
    return lax.rem(s[axis] + d[0], 4) * 2 + lax.rem(s[axis + 1] + d[1], 2)


def gram_rows(s, d, side):
    return (s[4] if side == 0 else 1 - s[4]) * 8 + group_spot(s, 2, d)


def gram_part(me, matrix, blocks, dists, prev=None, tile=512):
    n, cols, width = len(blocks), matrix.shape[1], blocks[0].shape[1]
    sides = [(d, side) for d in dists for side in (0, 1)]
    ins = [pl.BlockSpec((BLK, tile), lambda i, s, d=d, e=e: (gram_rows(s, d, e), i)) for d, e in sides]
    ins += [pl.BlockSpec((BLK, width), lambda i, s: (0, 0))] * n
    args = [matrix] * n + list(blocks)
    if prev is not None:
        ins.append(pl.BlockSpec((tile, width), lambda i, s: (i, 0)))
        args.append(prev)
    return pl.pallas_call(
        functools.partial(gram_kernel, n, int(prev is not None)),
        out_shape=jax.ShapeDtypeStruct((cols, width), F32),
        grid_spec=pltpu.PrefetchScalarGridSpec(
            num_scalar_prefetch=1,
            grid=(cols // tile,),
            in_specs=ins,
            out_specs=pl.BlockSpec((tile, width), lambda i, s: (i, 0)),
            scratch_shapes=[pltpu.VMEM((n * BLK, width), BF16)] * 2,
        ),
        cost_estimate=pl.CostEstimate(
            flops=6 * n * BLK * cols * width, transcendentals=0, bytes_accessed=4 * n * BLK * (cols + width)
        ),
    )(me, *args)


def gram_last_kernel(n, me, *refs):
    m, c, prev = refs[:n], refs[n : 2 * n], refs[2 * n]
    outs = refs[2 * n + 1 : 2 * n + 1 + len(REL)]
    acc = refs[-1]
    mh, ml = split(jnp.concatenate([r[...] for r in m], 0))
    ch, cl = split(jnp.concatenate([r[...] for r in c], 0))
    acc[...] = prev[...] + three(mh, ml, ch, cl, ((0,), (0,)))
    for out, d in zip(outs, REL):
        out[...] = acc[pl.ds(pl.multiple_of(group_spot(me, 0, d) * BLK, BLK), BLK), :]


def gram_last(me, matrix, blocks, dists, prev):
    n, cols, width = len(blocks), matrix.shape[1], blocks[0].shape[1]
    sides = [(d, side) for d in dists for side in (0, 1)]
    ins = [pl.BlockSpec((BLK, cols), lambda i, s, d=d, e=e: (gram_rows(s, d, e), 0)) for d, e in sides]
    ins += [pl.BlockSpec((BLK, width), lambda i, s: (0, 0))] * n + [pl.BlockSpec((cols, width), lambda i, s: (0, 0))]
    return pl.pallas_call(
        functools.partial(gram_last_kernel, n),
        out_shape=tuple([jax.ShapeDtypeStruct((BLK, width), F32)] * len(REL)),
        grid_spec=pltpu.PrefetchScalarGridSpec(
            num_scalar_prefetch=1,
            grid=(1,),
            in_specs=ins,
            out_specs=tuple([pl.BlockSpec((BLK, width), lambda i, s: (0, 0))] * len(REL)),
            scratch_shapes=[pltpu.VMEM((cols, width), F32)],
        ),
        cost_estimate=pl.CostEstimate(
            flops=6 * n * BLK * cols * width, transcendentals=0, bytes_accessed=4 * n * BLK * (cols + width)
        ),
    )(me, *([matrix] * n), *blocks, prev)


def product_kernel(n, has_prev, me, *refs):
    m, f, rest = refs[:n], refs[n : 2 * n], refs[2 * n :]
    out, fh, fl = rest[has_prev:]
    join_split(f, fh, fl)
    mh, ml = split(jnp.concatenate([r[...] for r in m], 1))
    made = three(mh, ml, fh[...], fl[...], ((1,), (0,)))
    out[...] = made + rest[0][...] if has_prev else made


def product_part(me, matrix, blocks, dists, prev=None, side=None, tile=512):
    n, width = len(blocks), blocks[0].shape[1]
    rows = matrix.shape[0] if side is None else matrix.shape[0] // 2
    steps = rows // tile

    def base(s):
        return 0 if side is None else (s[4] if side == 0 else 1 - s[4]) * steps

    ins = [pl.BlockSpec((tile, BLK), lambda i, s, d=d: (base(s) + i, group_spot(s, 0, d))) for d in dists]
    ins += [pl.BlockSpec((BLK, width), lambda i, s: (0, 0))] * n
    args = [matrix] * n + list(blocks)
    if prev is not None:
        ins.append(pl.BlockSpec((tile, width), lambda i, s: (base(s) + i, 0)))
        args.append(prev)
    return pl.pallas_call(
        functools.partial(product_kernel, n, int(prev is not None)),
        out_shape=jax.ShapeDtypeStruct((rows, width), F32),
        grid_spec=pltpu.PrefetchScalarGridSpec(
            num_scalar_prefetch=1,
            grid=(steps,),
            in_specs=ins,
            out_specs=pl.BlockSpec((tile, width), lambda i, s: (i, 0)),
            scratch_shapes=[pltpu.VMEM((n * BLK, width), BF16)] * 2,
        ),
        cost_estimate=pl.CostEstimate(
            flops=6 * n * BLK * rows * width, transcendentals=0, bytes_accessed=4 * rows * (n * BLK + width)
        ),
    )(me, *args)


def ring(v, axes, by):
    return lax.ppermute(v, axes[0], [(i, (i + by) % 4) for i in range(4)])


def flip(v, axis):
    return lax.ppermute(v, axis, [(0, 1), (1, 0)])


def at(axes, da, db):
    return (lax.axis_index(axes[0]) + da) % 4 * 2 + (lax.axis_index(axes[1]) + db) % 2


def spread(block, axes):
    n = block.shape[0] // 2
    p, m, z = ring(block, axes, 1), ring(block, axes, -1), flip(block, axes[1])
    pz = ring(z, axes, 1)
    m2 = ring(m, axes, -1)
    mz = flip(m, axes[1])
    u = ring(pz[:n], axes, 1)
    w = ring(mz[n:], axes, -1)
    return [
        ((0, 0), block), ((3, 0), p), ((1, 0), m), ((0, 1), z), ((3, 1), pz), ((2, 0), m2), ((1, 1), mz),
        ((2, 1), jnp.concatenate([u, w], 0)),
    ]


def scatter_sum(blk, axes):
    far = blk(2, 1)
    n = far.shape[0] // 2
    u, w = ring(far[:n], axes, -1), ring(far[n:], axes, 1)
    sp, tm = ring(blk(2, 0), axes, 1), ring(blk(3, 0), axes, -1)
    none = jnp.zeros_like(u)
    sz = flip(blk(1, 1) + jnp.concatenate([none, w], 0), axes[1])
    sm = ring(blk(3, 1) + jnp.concatenate([u, none], 0), axes, -1)
    tp = ring(blk(1, 0) + sz + sp, axes, 1)
    tz = flip(blk(0, 1) + sm, axes[1])
    return blk(0, 0) + tm + tp + tz


SPREAD_X = {0: 2, 1: 3, 3: 1, 2: 0}


def turn(v):
    perm = []
    for x in range(4):
        for zh in range(2):
            for y in range(4):
                for zl in range(2):
                    for c in range(2):
                        src = (((x * 2 + zh) * 4 + y) * 2 + zl) * 2 + c
                        dst = ((((x + SPREAD_X[(y - x) % 4]) % 4 * 2 + zl) * 4 + x) * 2 + zh) * 2 + c
                        perm.append((src, dst))
    return lax.ppermute(v, ALL, perm)


def per_device(matrix, factor_inverse, panel, split_index):
    rows_loc, cols_loc = matrix.shape
    width = factor_inverse.shape[0]
    x, zh = lax.axis_index("x"), lax.axis_index("zh")
    y, zl, core = lax.axis_index("y"), lax.axis_index("zl"), lax.axis_index("core")
    row, chip = x * 2 + zh, y * 2 + zl
    col = chip * 2 + core
    order = cols_loc * 16
    half = rows_loc // 2
    start = panel[0] * width
    owner = start // cols_loc
    offset = start - owner * cols_loc

    first = col * cols_loc + row * BLK - start
    inside = (first >= 0) & (first < width)
    inv_rows = lax.dynamic_slice_in_dim(factor_inverse, jnp.clip(first, 0, width - BLK), BLK, 1).T
    inv_rows = jnp.where(inside, inv_rows, F32(0.0))
    rows_global = row * rows_loc + core * half + chip * BLK + jnp.arange(BLK, dtype=jnp.int32)
    keep_rows = (rows_global < order // 2) == (rows_global < split_index[0])
    diag = (rows_global[:, None] == start + jnp.arange(width, dtype=jnp.int32)[None, :]).astype(F32)

    raw = {}
    for da, db in REL:
        j = at(GRID, da, db)
        got = flip(lax.dynamic_slice(matrix, ((1 - core) * half + j * BLK, offset), (BLK, width)), "core")
        kept = lax.dynamic_slice(matrix, (core * half + j * BLK, offset), (BLK, width))
        raw[da, db] = jnp.where(owner // 2 == chip, jnp.where(owner % 2 == core, kept, got), F32(0.0))
    block = scatter_sum(lambda da, db: raw[da, db], GRID)
    block = lax.dot_general(
        block, factor_inverse, (((1,), (1,)), ((), ())), precision=lax.Precision.HIGHEST, preferred_element_type=F32
    )

    me = jnp.stack([x, zh, y, zl, core]).astype(jnp.int32)
    own = [(d, got, flip(got, "core")) for d, got in spread(block, GRID)]

    def both(part):
        return [v for _, p, q in part for v in (p, q)], [d for d, _, _ in part]

    partial = gram_part(me, matrix, *both(own[:4]))
    partial = gram_part(me, matrix, *both(own[4:7]), partial)
    pieces = gram_last(me, matrix, *both(own[7:]), partial)
    parts = dict(zip(REL, pieces))
    block = scatter_sum(lambda da, db: parts[da, db], ROW) / order + inv_rows

    factor = spread(block, ROW)
    blocks, dists = [got for _, got in factor], [d for d, _ in factor]
    partial = product_part(me, matrix, blocks[:4], dists[:4])
    give = product_part(me, matrix, blocks[4:], dists[4:], partial, 1)
    got = flip(give, "core")
    kept = product_part(me, matrix, blocks[4:], dists[4:], partial, 0)

    def held(da, db):
        j = at(GRID, da, db) * BLK
        return lax.dynamic_slice_in_dim(kept, j, BLK, 0) + lax.dynamic_slice_in_dim(got, j, BLK, 0)

    total = scatter_sum(held, GRID)
    block = jnp.where(keep_rows[:, None], 0.5 * (diag + total), F32(0.0))

    out = jnp.zeros((8 * BLK, width), F32)
    for (da, db), got in spread(turn(block), ROW):
        sx, szh = (x + da) % 4, (zh + db) % 2
        d = sum(jnp.where((y + g) % 4 == sx, k, 0) for k, g in SPREAD_X.items())
        out = lax.dynamic_update_slice_in_dim(out, got, ((y + d) % 4 * 2 + szh) * BLK, 0)
    return out


def solution(mesh):
    fine = Mesh(mesh.devices.reshape(SIZES), ALL)
    placed = (P(ROW, COL), P(), P(), P())

    return jax.shard_map(per_device, mesh=fine, in_specs=placed, out_specs=P(COL, None), check_vma=False)
```

profile of v0, /device:TPU:0, one launch (start us, length us, event | category | flops | bytes accessed | tf_op | source)
XLA Modules:
  0.0 241.2 jit_solution(3935774521635435833)
XLA Ops:
  13.4 3.4 %collective-permute-done.6 = f32[64,512]{1,0:T(8,128)} collective-permute-done((f32[64,512]{1,0:T(8,128)}, f32[64,512]{1,0:T(8,128)}, u32[]{:S(2)}, u32[]{:S(2)}) %collective-permute-start.6) | collective-permute-done | bytes 131104 | tf_op jit(solution)/shard_map/ppermute | solution.py:155
  32.4 6.8 %collective-permute-done.10 = f32[128,512]{1,0:T(8,128)S(1)} collective-permute-done((f32[128,512]{1,0:T(8,128)}, f32[128,512]{1,0:T(8,128)S(1)}, u32[]{:S(2)}, u32[]{:S(2)}) %collective-permute-start.10) | collective-permute-done | bytes 262176 | tf_op jit(solution)/shard_map/ppermute | solution.py:155
  44.2 5.4 %collective-permute-done.16.refs_14_ = f32[128,512]{1,0:T(8,128)S(1)} collective-permute-done((f32[128,512]{1,0:T(8,128)S(1)}, f32[128,512]{1,0:T(8,128)S(1)}, u32[]{:S(2)}, u32[]{:S(2)}) %collective-permute-start.16) | collective-permute-done | bytes 262176 | tf_op jit(solution)/shard_map/ppermute | solution.py:159
  50.1 7.7 %collective-permute-done.17.refs_6_ = f32[128,512]{1,0:T(8,128)S(1)} collective-permute-done((f32[128,512]{1,0:T(8,128)S(1)}, f32[128,512]{1,0:T(8,128)S(1)}, u32[]{:S(2)}, u32[]{:S(2)}) %collective-permute-start.17) | collective-permute-done | bytes 262176 | tf_op jit(solution)/shard_map/ppermute | solution.py:155
  57.9 3.3 %collective-permute-start.21 = (f32[64,512]{1,0:T(8,128)S(1)}, f32[64,512]{1,0:T(8,128)}, u32[]{:S(2)}, u32[]{:S(2)}) collective-permute-start(f32[64,512]{1,0:T(8,128)S(1)} %slice.51), channel_id=1, source_target_pairs={{0,12},{4,0},{8,4},{12,8},{1,13},{5,1},{9,5},{13,9},{2,14},{6,2},{... | collective-permute-start | bytes 393224 | tf_op jit(solution)/shard_map/ppermute | solution.py:155
  70.5 8.0 %shard_map.46.refs_12_ = f32[1024,512]{1,0:T(8,128)} custom-call(s32[5]{0:T(128)} %stack.23.me, f32[2048,1024]{1,0:T(8,128)} %refs_3_.9, f32[2048,1024]{1,0:T(8,128)} %refs_3_.9, f32[2048,1024]{1,0:T(8,128)} %refs_3_.9, f32[2048,1024]{1,0:T(8,128)} %refs_3_.9, f32[2048,1024]{1,0:T(8,128)} %refs_3_.9, f32[2048,1024]{1,0:T(8,128)} %refs_3_.9, ...), custom_call_target="tpu_custom_call" | custom-call | flops 3221225472 | bytes 6291456 | tf_op jit(solution)/shard_map/pallas_call | solution.py:67
  78.6 7.1 %shard_map.47.refs_4_ = f32[1024,512]{1,0:T(8,128)} custom-call(s32[5]{0:T(128)} %stack.23.me, f32[2048,1024]{1,0:T(8,128)} %refs_3_.9, f32[2048,1024]{1,0:T(8,128)} %refs_3_.9, f32[2048,1024]{1,0:T(8,128)} %refs_3_.9, f32[2048,1024]{1,0:T(8,128)} %refs_3_.9, f32[2048,1024]{1,0:T(8,128)} %refs_3_.9, f32[2048,1024]{1,0:T(8,128)} %refs_3_.9, ...), custom_call_target="tpu_custom_call" | custom-call | flops 2415919104 | bytes 4718592 | tf_op jit(solution)/shard_map/pallas_call | solution.py:67
  85.8 5.1 %shard_map.48 = (f32[128,512]{1,0:T(8,128)}, f32[128,512]{1,0:T(8,128)}, f32[128,512]{1,0:T(8,128)}, f32[128,512]{1,0:T(8,128)}, f32[128,512]{1,0:T(8,128)}, /*i...) custom-call(s32[5]{0:T(128)} %stack.23.me, f32[2048,1024]{1,0:T(8,128)} %refs_3_.9, f32[2048,1024]{1,0:T(8,128)} %refs_3_.9, ...), custom_call_target="tpu_custom_call" | custom-call | flops 805306368 | bytes 1572864 | tf_op jit(solution)/shard_map/pallas_call | solution.py:99
  100.6 3.7 %collective-permute-start.34 = (f32[128,512]{1,0:T(8,128)S(1)}, f32[128,512]{1,0:T(8,128)S(1)}, u32[]{:S(2)}, u32[]{:S(2)}) collective-permute-start(f32[128,512]{1,0:T(8,128)S(1)} %pad_add_fusion.3), channel_id=1, source_target_pairs={{0,16},{16,0},{1,17},{17,1},{2,18},{18,2},{3,19},{19,3},{4,20},{20... | collective-permute-start | bytes 786440 | tf_op jit(solution)/shard_map/ppermute | solution.py:159
  110.8 3.7 %collective-permute-done.38 = f32[128,512]{1,0:T(8,128)S(1)} collective-permute-done((f32[128,512]{1,0:T(8,128)S(1)}, f32[128,512]{1,0:T(8,128)S(1)}, u32[]{:S(2)}, u32[]{:S(2)}) %collective-permute-start.38) | collective-permute-done | bytes 262176 | tf_op jit(solution)/shard_map/ppermute | solution.py:155
  118.1 6.2 %collective-permute-done.39 = f32[128,512]{1,0:T(8,128)S(1)} collective-permute-done((f32[128,512]{1,0:T(8,128)S(1)}, f32[128,512]{1,0:T(8,128)S(1)}, u32[]{:S(2)}, u32[]{:S(2)}) %collective-permute-start.39) | collective-permute-done | bytes 262176 | tf_op jit(solution)/shard_map/ppermute | solution.py:159
  127.3 7.6 %collective-permute-done.40.refs_7_ = f32[128,512]{1,0:T(8,128)S(1)} collective-permute-done((f32[128,512]{1,0:T(8,128)S(1)}, f32[128,512]{1,0:T(8,128)S(1)}, u32[]{:S(2)}, u32[]{:S(2)}) %collective-permute-start.40) | collective-permute-done | bytes 262176 | tf_op jit(solution)/shard_map/ppermute | solution.py:159
  137.2 3.7 %collective-permute-start.43 = (f32[128,512]{1,0:T(8,128)S(1)}, f32[128,512]{1,0:T(8,128)S(1)}, u32[]{:S(2)}, u32[]{:S(2)}) collective-permute-start(f32[128,512]{1,0:T(8,128)S(1)} %collective-permute-done.42.refs_6_), channel_id=1, source_target_pairs={{0,96},{32,0},{64,32},{96,64},{1,97},{33,1},{65,33},{97,65},{2,98}... | collective-permute-start | bytes 786440 | tf_op jit(solution)/shard_map/ppermute | solution.py:155
  142.9 3.4 %collective-permute-start.46 = (f32[64,512]{1,0:T(8,128)S(1)}, f32[64,512]{1,0:T(8,128)S(1)}, u32[]{:S(2)}, u32[]{:S(2)}) collective-permute-start(f32[64,512]{1,0:T(8,128)S(1)} %slice.53), channel_id=1, source_target_pairs={{0,96},{32,0},{64,32},{96,64},{1,97},{33,1},{65,33},{97,65},{2,98}... | collective-permute-start | bytes 393224 | tf_op jit(solution)/shard_map/ppermute | solution.py:155
  147.1 8.2 %shard_map.49.refs_8_ = f32[2048,512]{1,0:T(8,128)} custom-call(s32[5]{0:T(128)} %stack.23.me, f32[2048,1024]{1,0:T(8,128)} %refs_3_.9, f32[2048,1024]{1,0:T(8,128)} %refs_3_.9, f32[2048,1024]{1,0:T(8,128)} %refs_3_.9, f32[2048,1024]{1,0:T(8,128)} %refs_3_.9, f32[128,512]{1,0:T(8,128)} %copy-done.7, f32[128,512]{1,0:T(8,128)} %copy-done.18, ...), custom_call_target="tpu_custom_call" | custom-call | flops 3221225472 | bytes 8388608 | tf_op jit(solution)/shard_map/pallas_call | solution.py:138
  156.8 5.8 %shard_map.51 = f32[1024,512]{1,0:T(8,128)} custom-call(s32[5]{0:T(128)} %stack.23.me, f32[2048,1024]{1,0:T(8,128)} %refs_3_.9, f32[2048,1024]{1,0:T(8,128)} %refs_3_.9, f32[2048,1024]{1,0:T(8,128)} %refs_3_.9, f32[2048,1024]{1,0:T(8,128)} %refs_3_.9, f32[128,512]{1,0:T(8,128)} %copy-done.2, f32[128,512]{1,0:T(8,128)} %copy-done.5, f32[128,512]{1,0:T(8,128)} %copy-done.3, ...), custom_call_target="tpu_custom_call" | custom-call | flops 1610612736 | bytes 4194304 | tf_op jit(solution)/shard_map/pallas_call | solution.py:138
  162.6 5.8 %shard_map.50 = f32[1024,512]{1,0:T(8,128)} custom-call(s32[5]{0:T(128)} %stack.23.me, f32[2048,1024]{1,0:T(8,128)} %refs_3_.9, f32[2048,1024]{1,0:T(8,128)} %refs_3_.9, f32[2048,1024]{1,0:T(8,128)} %refs_3_.9, f32[2048,1024]{1,0:T(8,128)} %refs_3_.9, f32[128,512]{1,0:T(8,128)} %copy-done.2, f32[128,512]{1,0:T(8,128)} %copy-done.5, f32[128,512]{1,0:T(8,128)} %copy-done.3, ...), custom_call_target="tpu_custom_call" | custom-call | flops 1610612736 | bytes 4194304 | tf_op jit(solution)/shard_map/pallas_call | solution.py:138
  172.7 3.9 %collective-permute-done.50 = f32[64,512]{1,0:T(8,128)S(1)} collective-permute-done((f32[64,512]{1,0:T(8,128)S(1)}, f32[64,512]{1,0:T(8,128)S(1)}, u32[]{:S(2)}, u32[]{:S(2)}) %collective-permute-start.50) | collective-permute-done | bytes 131104 | tf_op jit(solution)/shard_map/ppermute | solution.py:155
  196.1 3.5 %collective-permute-done.53 = f32[128,512]{1,0:T(8,128)} collective-permute-done((f32[128,512]{1,0:T(8,128)}, f32[128,512]{1,0:T(8,128)}, u32[]{:S(2)}, u32[]{:S(2)}) %collective-permute-start.53) | collective-permute-done | bytes 262176 | tf_op jit(solution)/shard_map/ppermute | solution.py:155
  202.6 9.3 %collective-permute-done.57 = f32[128,512]{1,0:T(8,128)S(1)} collective-permute-done((f32[128,512]{1,0:T(8,128)S(1)}, f32[128,512]{1,0:T(8,128)S(1)}, u32[]{:S(2)}, u32[]{:S(2)}) %collective-permute-start.57) | collective-permute-done | bytes 262176 | tf_op jit(solution)/shard_map/ppermute | solution.py:206
  211.9 4.8 %collective-permute-start.59 = (f32[128,512]{1,0:T(8,128)S(1)}, f32[128,512]{1,0:T(8,128)S(1)}, u32[]{:S(2)}, u32[]{:S(2)}) collective-permute-start(f32[128,512]{1,0:T(8,128)S(1)} %collective-permute-done.57), channel_id=1, source_target_pairs={{0,96},{32,0},{64,32},{96,64},{1,97},{33,1},{65,33},{97,65},{2,98}... | collective-permute-start | bytes 786440 | tf_op jit(solution)/shard_map/ppermute | solution.py:155
  221.2 3.7 %collective-permute-start.62 = (f32[128,512]{1,0:T(8,128)S(1)}, f32[128,512]{1,0:T(8,128)S(1)}, u32[]{:S(2)}, u32[]{:S(2)}) collective-permute-start(f32[128,512]{1,0:T(8,128)S(1)} %collective-permute-done.59), channel_id=1, source_target_pairs={{0,96},{32,0},{64,32},{96,64},{1,97},{33,1},{65,33},{97,65},{2,98}... | collective-permute-start | bytes 786440 | tf_op jit(solution)/shard_map/ppermute | solution.py:155
  226.7 7.5 %collective-permute-done.61 = f32[128,512]{1,0:T(8,128)S(1)} collective-permute-done((f32[128,512]{1,0:T(8,128)S(1)}, f32[128,512]{1,0:T(8,128)S(1)}, u32[]{:S(2)}, u32[]{:S(2)}) %collective-permute-start.61) | collective-permute-done | bytes 262176 | tf_op jit(solution)/shard_map/ppermute | solution.py:155
  234.3 3.3 %collective-permute-start.65 = (f32[64,512]{1,0:T(8,128)S(1)}, f32[64,512]{1,0:T(8,128)S(1)}, u32[]{:S(2)}, u32[]{:S(2)}) collective-permute-start(f32[64,512]{1,0:T(8,128)S(1)} %slice.57), channel_id=1, source_target_pairs={{0,96},{32,0},{64,32},{96,64},{1,97},{33,1},{65,33},{97,65},{2,98}... | collective-permute-start | bytes 393224 | tf_op jit(solution)/shard_map/ppermute | solution.py:155
  (198 shorter events, 108.2 us)
Async XLA Ops:
  10.1 12.9 %collective-permute-start.11 = (f32[128,512]{1,0:T(8,128)S(1)}, f32[128,512]{1,0:T(8,128)}, u32[]{:S(2)}, u32[]{:S(2)}) collective-permute-start(f32[128,512]{1,0:T(8,128)S(1)} %get-tuple-element.23), channel_id=1, source_target_pairs={{0,1},{1,0},{2,3},{3,2},{4,5},{5,4},{6,7},{7,6},{8,9},{9,8},{10,11... | collective-permute-start | bytes 786440 | tf_op jit(solution)/shard_map/ppermute | solution.py:159
  10.2 12.8 %collective-permute-start.3 = (f32[128,512]{1,0:T(8,128)S(1)}, f32[128,512]{1,0:T(8,128)S(1)}, u32[]{:S(2)}, u32[]{:S(2)}) collective-permute-start(f32[128,512]{1,0:T(8,128)S(1)} %get-tuple-element.27), channel_id=1, source_target_pairs={{0,1},{1,0},{2,3},{3,2},{4,5},{5,4},{6,7},{7,6},{8,9},{9,8},{10,11... | collective-permute-start | bytes 786440 | tf_op jit(solution)/shard_map/ppermute | solution.py:159
  23.0 9.4 %collective-permute-start = (f32[128,512]{1,0:T(8,128)S(1)}, f32[128,512]{1,0:T(8,128)S(1)}, u32[]{:S(2)}, u32[]{:S(2)}) collective-permute-start(f32[128,512]{1,0:T(8,128)S(1)} %get-tuple-element.21), channel_id=1, source_target_pairs={{0,1},{1,0},{2,3},{3,2},{4,5},{5,4},{6,7},{7,6},{8,9},{9,8},{10,11... | collective-permute-start | bytes 786440 | tf_op jit(solution)/shard_map/ppermute | solution.py:159
  23.0 9.4 %collective-permute-start.2 = (f32[128,512]{1,0:T(8,128)S(1)}, f32[128,512]{1,0:T(8,128)S(1)}, u32[]{:S(2)}, u32[]{:S(2)}) collective-permute-start(f32[128,512]{1,0:T(8,128)S(1)} %get-tuple-element.29), channel_id=1, source_target_pairs={{0,12},{4,0},{8,4},{12,8},{1,13},{5,1},{9,5},{13,9},{2,14},{6,2},{... | collective-permute-start | bytes 786440 | tf_op jit(solution)/shard_map/ppermute | solution.py:155
  50.1 11.1 %collective-permute-start.28 = (f32[128,512]{1,0:T(8,128)S(1)}, f32[128,512]{1,0:T(8,128)S(1)}, u32[]{:S(2)}, u32[]{:S(2)}) collective-permute-start(f32[128,512]{1,0:T(8,128)S(1)} %fusion.refs_8_), channel_id=1, source_target_pairs={{0,4},{4,8},{8,12},{12,0},{1,5},{5,9},{9,13},{13,1},{2,6},{6,10},{... | collective-permute-start | bytes 786440 | tf_op jit(solution)/shard_map/ppermute | solution.py:155
  66.6 12.0 %collective-permute-start.23 = (f32[128,512]{1,0:T(8,128)S(1)}, f32[128,512]{1,0:T(8,128)}, u32[]{:S(2)}, u32[]{:S(2)}) collective-permute-start(f32[128,512]{1,0:T(8,128)S(1)} %collective-permute-done.17.refs_6_), channel_id=1, source_target_pairs={{0,1},{1,0},{2,3},{3,2},{4,5},{5,4},{6,7},{7,6},{8,9},{9,8},{10,11... | collective-permute-start | bytes 786440 | tf_op jit(solution)/shard_map/ppermute | solution.py:159
  67.2 11.4 %collective-permute-start.26 = (f32[128,512]{1,0:T(8,128)S(1)}, f32[128,512]{1,0:T(8,128)}, u32[]{:S(2)}, u32[]{:S(2)}) collective-permute-start(f32[128,512]{1,0:T(8,128)S(1)} %collective-permute-done.20.refs_10_), channel_id=1, source_target_pairs={{0,1},{1,0},{2,3},{3,2},{4,5},{5,4},{6,7},{7,6},{8,9},{9,8},{10,11... | collective-permute-start | bytes 786440 | tf_op jit(solution)/shard_map/ppermute | solution.py:159
  70.0 15.8 %collective-permute-start.22 = (f32[128,512]{1,0:T(8,128)S(1)}, f32[128,512]{1,0:T(8,128)}, u32[]{:S(2)}, u32[]{:S(2)}) collective-permute-start(f32[128,512]{1,0:T(8,128)S(1)} %constant_dynamic-update-slice_fusion.refs_2_), channel_id=1, source_target_pairs={{0,1},{1,0},{2,3},{3,2},{4,5},{5,4},{6,7},{7,6},{8,9},{9,8},{10,11... | collective-permute-start | bytes 786440 | tf_op jit(solution)/shard_map/ppermute | solution.py:159
  93.5 14.2 %collective-permute-start.35 = (f32[128,512]{1,0:T(8,128)}, f32[128,512]{1,0:T(8,128)S(1)}, u32[]{:S(2)}, u32[]{:S(2)}) collective-permute-start(f32[128,512]{1,0:T(8,128)} %get-tuple-element.18), channel_id=1, source_target_pairs={{0,32},{32,64},{64,96},{96,0},{1,33},{33,65},{65,97},{97,1},{2,34}... | collective-permute-start | bytes 786440 | tf_op jit(solution)/shard_map/ppermute | solution.py:155
  95.0 9.3 %collective-permute-start.37 = (f32[64,512]{1,0:T(8,128)S(1)}, f32[64,512]{1,0:T(8,128)S(1)}, u32[]{:S(2)}, u32[]{:S(2)}) collective-permute-start(f32[64,512]{1,0:T(8,128)S(1)} %get-tuple-element.44), channel_id=1, source_target_pairs={{0,96},{32,0},{64,32},{96,64},{1,97},{33,1},{65,33},{97,65},{2,98}... | collective-permute-start | bytes 393224 | tf_op jit(solution)/shard_map/ppermute | solution.py:155
  106.9 10.7 %collective-permute-start.32 = (f32[128,512]{1,0:T(8,128)}, f32[128,512]{1,0:T(8,128)S(1)}, u32[]{:S(2)}, u32[]{:S(2)}) collective-permute-start(f32[128,512]{1,0:T(8,128)} %get-tuple-element.14), channel_id=1, source_target_pairs={{0,96},{32,0},{64,32},{96,64},{1,97},{33,1},{65,33},{97,65},{2,98}... | collective-permute-start | bytes 786440 | tf_op jit(solution)/shard_map/ppermute | solution.py:155
  114.5 9.8 %collective-permute-start.39 = (f32[128,512]{1,0:T(8,128)S(1)}, f32[128,512]{1,0:T(8,128)S(1)}, u32[]{:S(2)}, u32[]{:S(2)}) collective-permute-start(f32[128,512]{1,0:T(8,128)S(1)} %add.716), channel_id=1, source_target_pairs={{0,16},{16,0},{1,17},{17,1},{2,18},{18,2},{3,19},{19,3},{4,20},{20... | collective-permute-start | bytes 786440 | tf_op jit(solution)/shard_map/ppermute | solution.py:159
  124.4 10.5 %collective-permute-start.40 = (f32[128,512]{1,0:T(8,128)S(1)}, f32[128,512]{1,0:T(8,128)S(1)}, u32[]{:S(2)}, u32[]{:S(2)}) collective-permute-start(f32[128,512]{1,0:T(8,128)S(1)} %bitcast_add_fusion.refs_4_), channel_id=1, source_target_pairs={{0,16},{16,0},{1,17},{17,1},{2,18},{18,2},{3,19},{19,3},{4,20},{20... | collective-permute-start | bytes 786440 | tf_op jit(solution)/shard_map/ppermute | solution.py:159
  124.5 10.4 %collective-permute-start.42 = (f32[128,512]{1,0:T(8,128)S(1)}, f32[128,512]{1,0:T(8,128)S(1)}, u32[]{:S(2)}, u32[]{:S(2)}) collective-permute-start(f32[128,512]{1,0:T(8,128)S(1)} %bitcast_add_fusion.refs_4_), channel_id=1, source_target_pairs={{0,96},{32,0},{64,32},{96,64},{1,97},{33,1},{65,33},{97,65},{2,98}... | collective-permute-start | bytes 786440 | tf_op jit(solution)/shard_map/ppermute | solution.py:155
  137.2 18.2 %collective-permute-start.43 = (f32[128,512]{1,0:T(8,128)S(1)}, f32[128,512]{1,0:T(8,128)S(1)}, u32[]{:S(2)}, u32[]{:S(2)}) collective-permute-start(f32[128,512]{1,0:T(8,128)S(1)} %collective-permute-done.42.refs_6_), channel_id=1, source_target_pairs={{0,96},{32,0},{64,32},{96,64},{1,97},{33,1},{65,33},{97,65},{2,98}... | collective-permute-start | bytes 786440 | tf_op jit(solution)/shard_map/ppermute | solution.py:155
  142.5 12.8 %collective-permute-start.45 = (f32[64,512]{1,0:T(8,128)S(1)}, f32[64,512]{1,0:T(8,128)S(1)}, u32[]{:S(2)}, u32[]{:S(2)}) collective-permute-start(f32[64,512]{1,0:T(8,128)S(1)} %slice.52), channel_id=1, source_target_pairs={{0,32},{32,64},{64,96},{96,0},{1,33},{33,65},{65,97},{97,1},{2,34}... | collective-permute-start | bytes 393224 | tf_op jit(solution)/shard_map/ppermute | solution.py:155
  142.9 12.4 %collective-permute-start.46 = (f32[64,512]{1,0:T(8,128)S(1)}, f32[64,512]{1,0:T(8,128)S(1)}, u32[]{:S(2)}, u32[]{:S(2)}) collective-permute-start(f32[64,512]{1,0:T(8,128)S(1)} %slice.53), channel_id=1, source_target_pairs={{0,96},{32,0},{64,32},{96,64},{1,97},{33,1},{65,33},{97,65},{2,98}... | collective-permute-start | bytes 393224 | tf_op jit(solution)/shard_map/ppermute | solution.py:155
  178.8 9.4 %collective-permute-start.52 = (f32[128,512]{1,0:T(8,128)}, f32[128,512]{1,0:T(8,128)}, u32[]{:S(2)}, u32[]{:S(2)}) collective-permute-start(f32[128,512]{1,0:T(8,128)} %get-tuple-element.37), channel_id=1, source_target_pairs={{0,4},{4,8},{8,12},{12,0},{1,5},{5,9},{9,13},{13,1},{2,6},{6,10},{... | collective-permute-start | bytes 786440 | tf_op jit(solution)/shard_map/ppermute | solution.py:155
  179.9 9.5 %collective-permute-start.55 = (f32[128,512]{1,0:T(8,128)}, f32[128,512]{1,0:T(8,128)}, u32[]{:S(2)}, u32[]{:S(2)}) collective-permute-start(f32[128,512]{1,0:T(8,128)} %get-tuple-element.36), channel_id=1, source_target_pairs={{0,12},{4,0},{8,4},{12,8},{1,13},{5,1},{9,5},{13,9},{2,14},{6,2},{... | collective-permute-start | bytes 786440 | tf_op jit(solution)/shard_map/ppermute | solution.py:155
  182.0 14.1 %collective-permute-start.49 = (f32[128,512]{1,0:T(8,128)S(1)}, f32[128,512]{1,0:T(8,128)}, u32[]{:S(2)}, u32[]{:S(2)}) collective-permute-start(f32[128,512]{1,0:T(8,128)S(1)} %get-tuple-element.35), channel_id=1, source_target_pairs={{0,12},{4,0},{8,4},{12,8},{1,13},{5,1},{9,5},{13,9},{2,14},{6,2},{... | collective-permute-start | bytes 786440 | tf_op jit(solution)/shard_map/ppermute | solution.py:155
  201.4 10.5 %collective-permute-start.57 = (f32[128,512]{1,0:T(8,128)S(1)}, f32[128,512]{1,0:T(8,128)S(1)}, u32[]{:S(2)}, u32[]{:S(2)}) collective-permute-start(f32[128,512]{1,0:T(8,128)S(1)} %multiply_select_fusion), channel_id=1, source_target_pairs={{0,64},{1,65},{2,80},{3,81},{4,96},{5,97},{6,112},{7,113},{8,0},{9... | collective-permute-start | bytes 786440 | tf_op jit(solution)/shard_map/ppermute | solution.py:206
  216.7 9.9 %collective-permute-start.60 = (f32[128,512]{1,0:T(8,128)S(1)}, f32[128,512]{1,0:T(8,128)S(1)}, u32[]{:S(2)}, u32[]{:S(2)}) collective-permute-start(f32[128,512]{1,0:T(8,128)S(1)} %collective-permute-done.57), channel_id=1, source_target_pairs={{0,16},{16,0},{1,17},{17,1},{2,18},{18,2},{3,19},{19,3},{4,20},{20... | collective-permute-start | bytes 786440 | tf_op jit(solution)/shard_map/ppermute | solution.py:159
  221.2 16.4 %collective-permute-start.62 = (f32[128,512]{1,0:T(8,128)S(1)}, f32[128,512]{1,0:T(8,128)S(1)}, u32[]{:S(2)}, u32[]{:S(2)}) collective-permute-start(f32[128,512]{1,0:T(8,128)S(1)} %collective-permute-done.59), channel_id=1, source_target_pairs={{0,96},{32,0},{64,32},{96,64},{1,97},{33,1},{65,33},{97,65},{2,98}... | collective-permute-start | bytes 786440 | tf_op jit(solution)/shard_map/ppermute | solution.py:155
  224.9 9.4 %collective-permute-start.63 = (f32[128,512]{1,0:T(8,128)S(1)}, f32[128,512]{1,0:T(8,128)S(1)}, u32[]{:S(2)}, u32[]{:S(2)}) collective-permute-start(f32[128,512]{1,0:T(8,128)S(1)} %collective-permute-done.59), channel_id=1, source_target_pairs={{0,16},{16,0},{1,17},{17,1},{2,18},{18,2},{3,19},{19,3},{4,20},{20... | collective-permute-start | bytes 786440 | tf_op jit(solution)/shard_map/ppermute | solution.py:159
  (63 other events, 611.2 us)
where the time goes:
time: 242 us; the launch traced here: 241 us
  waiting for transfers between devices  99.4 us (41%)
  starting transfers between devices  72.8 us (30%)
  Pallas kernels  40 us (17%)
  other arithmetic  16 us (7%)
  local copies, waits for them, and re-layouts  8.77 us (4%)
    ppermute x36, waiting for transfers between devices, ring(): return lax.ppermute(v, axes[0], [(i, (i + by) % 4) for i in range(4)])  64.4 us
    ppermute x36, starting transfers between devices, ring(): return lax.ppermute(v, axes[0], [(i, (i + by) % 4) for i in range(4)])  52.3 us
    ppermute x29, waiting for transfers between devices, flip(): return lax.ppermute(v, axis, [(0, 1), (1, 0)])  25.8 us
    pallas_call x3, Pallas kernels, product_part(): pl.pallas_call(functools.partial(product_kernel, n, int(prev is not None)...  19.8 us
    ppermute x29, starting transfers between devices, flip(): return lax.ppermute(v, axis, [(0, 1), (1, 0)])  19.3 us
    pallas_call x2, Pallas kernels, gram_part(): pl.pallas_call(functools.partial(gram_kernel, n, int(prev is not None)),...  15.2 us
    ppermute x1, waiting for transfers between devices, turn(): return lax.ppermute(v, ALL, perm)  9.29 us
    add x3, other arithmetic, scatter_sum(): tp = ring(blk(1, 0) + sz + sp, axes, 1)  5.25 us
  transfers between devices with their start and end apart: 66, of which 31 were waited for; matrix products, arithmetic and copies ran while one was open for 6% of the time, Pallas kernels for 12%

commit v1 on v0

--- a/solution.py
+++ b/solution.py
@@ -30,92 +30,57 @@
     return one(ah, bh) + (one(ah, bl) + one(al, bh))
 
 
-def join_split(refs, hi, lo):
+def group_spot(s, axis, d):
+    return lax.rem(s[axis] + d[0], 4) * 2 + lax.rem(s[axis + 1] + d[1], 2)
+
+
+def join_split(refs, spots, hi, lo):
     @pl.when(pl.program_id(0) == 0)
     def _():
-        for k, ref in enumerate(refs):
-            rows = pl.ds(k * BLK, BLK)
+        for ref, spot in zip(refs, spots):
+            rows = pl.ds(spot * BLK if isinstance(spot, int) else pl.multiple_of(spot * BLK, BLK), BLK)
             hi[rows, :], lo[rows, :] = split(ref[...])
 
 
-def gram_kernel(n, has_prev, me, *refs):
-    m, c, rest = refs[:n], refs[n : 2 * n], refs[2 * n :]
-    out, ch, cl = rest[has_prev:]
-    join_split(c, ch, cl)
-    mh, ml = split(jnp.concatenate([r[...] for r in m], 0))
+def gram_kernel(dists, pair, me, *refs):
+    n = 2 * len(dists)
+    m, c, outs, (ch, cl) = refs[:pair], refs[pair : pair + n], refs[pair + n : -2], refs[-2:]
+    spots = [side * 8 + group_spot(me, 2, d) for d in dists for side in (me[4], 1 - me[4])]
+    join_split(c, spots, ch, cl)
+    mh, ml = split(jnp.concatenate([r[...] for r in m], 1) if pair > 1 else m[0][...])
     made = three(mh, ml, ch[...], cl[...], ((0,), (0,)))
-    out[...] = made + rest[0][...] if has_prev else made
-
-
-def group_spot(s, axis, d):
-    return lax.rem(s[axis] + d[0], 4) * 2 + lax.rem(s[axis + 1] + d[1], 2)
-
-
-def gram_rows(s, d, side):
-    return (s[4] if side == 0 else 1 - s[4]) * 8 + group_spot(s, 2, d)
-
-
-def gram_part(me, matrix, blocks, dists, prev=None, tile=512):
-    n, cols, width = len(blocks), matrix.shape[1], blocks[0].shape[1]
-    sides = [(d, side) for d in dists for side in (0, 1)]
-    ins = [pl.BlockSpec((BLK, tile), lambda i, s, d=d, e=e: (gram_rows(s, d, e), i)) for d, e in sides]
-    ins += [pl.BlockSpec((BLK, width), lambda i, s: (0, 0))] * n
-    args = [matrix] * n + list(blocks)
-    if prev is not None:
-        ins.append(pl.BlockSpec((tile, width), lambda i, s: (i, 0)))
-        args.append(prev)
+    for k in range(len(outs)):
+
+        @pl.when(pl.program_id(0) == k // pair)
+        def _(k=k):
+            outs[k][...] = made[k % pair * BLK : (k % pair + 1) * BLK]
+
+
+def gram(me, matrix, blocks, dists, pair=2):
+    rows, width = matrix.shape[0], blocks[0].shape[1]
+
+    def column(i, s, e):
+        return sum(jnp.where(i == k // pair, group_spot(s, 0, d), 0) for k, d in enumerate(REL) if k % pair == e)
+
+    ins = [pl.BlockSpec((rows, BLK), lambda i, s, e=e: (0, column(i, s, e))) for e in range(pair)]
+    ins += [pl.BlockSpec((BLK, width), lambda i, s: (0, 0))] * len(blocks)
     return pl.pallas_call(
-        functools.partial(gram_kernel, n, int(prev is not None)),
-        out_shape=jax.ShapeDtypeStruct((cols, width), F32),
-        grid_spec=pltpu.PrefetchScalarGridSpec(
-            num_scalar_prefetch=1,
-            grid=(cols // tile,),
-            in_specs=ins,
-            out_specs=pl.BlockSpec((tile, width), lambda i, s: (i, 0)),
-            scratch_shapes=[pltpu.VMEM((n * BLK, width), BF16)] * 2,
-        ),
-        cost_estimate=pl.CostEstimate(
-            flops=6 * n * BLK * cols * width, transcendentals=0, bytes_accessed=4 * n * BLK * (cols + width)
-        ),
-    )(me, *args)
-
-
-def gram_last_kernel(n, me, *refs):
-    m, c, prev = refs[:n], refs[n : 2 * n], refs[2 * n]
-    outs = refs[2 * n + 1 : 2 * n + 1 + len(REL)]
-    acc = refs[-1]
-    mh, ml = split(jnp.concatenate([r[...] for r in m], 0))
-    ch, cl = split(jnp.concatenate([r[...] for r in c], 0))
-    acc[...] = prev[...] + three(mh, ml, ch, cl, ((0,), (0,)))
-    for out, d in zip(outs, REL):
-        out[...] = acc[pl.ds(pl.multiple_of(group_spot(me, 0, d) * BLK, BLK), BLK), :]
-
-
-def gram_last(me, matrix, blocks, dists, prev):
-    n, cols, width = len(blocks), matrix.shape[1], blocks[0].shape[1]
-    sides = [(d, side) for d in dists for side in (0, 1)]
-    ins = [pl.BlockSpec((BLK, cols), lambda i, s, d=d, e=e: (gram_rows(s, d, e), 0)) for d, e in sides]
-    ins += [pl.BlockSpec((BLK, width), lambda i, s: (0, 0))] * n + [pl.BlockSpec((cols, width), lambda i, s: (0, 0))]
-    return pl.pallas_call(
-        functools.partial(gram_last_kernel, n),
+        functools.partial(gram_kernel, dists, pair),
         out_shape=tuple([jax.ShapeDtypeStruct((BLK, width), F32)] * len(REL)),
         grid_spec=pltpu.PrefetchScalarGridSpec(
             num_scalar_prefetch=1,
-            grid=(1,),
+            grid=(len(REL) // pair,),
             in_specs=ins,
             out_specs=tuple([pl.BlockSpec((BLK, width), lambda i, s: (0, 0))] * len(REL)),
-            scratch_shapes=[pltpu.VMEM((cols, width), F32)],
+            scratch_shapes=[pltpu.VMEM((rows, width), BF16)] * 2,
         ),
-        cost_estimate=pl.CostEstimate(
-            flops=6 * n * BLK * cols * width, transcendentals=0, bytes_accessed=4 * n * BLK * (cols + width)
-        ),
-    )(me, *([matrix] * n), *blocks, prev)
+    )(me, *([matrix] * pair), *blocks)
 
 
 def product_kernel(n, has_prev, me, *refs):
     m, f, rest = refs[:n], refs[n : 2 * n], refs[2 * n :]
     out, fh, fl = rest[has_prev:]
-    join_split(f, fh, fl)
+    join_split(f, range(n), fh, fl)
     mh, ml = split(jnp.concatenate([r[...] for r in m], 1))
     made = three(mh, ml, fh[...], fl[...], ((1,), (0,)))
     out[...] = made + rest[0][...] if has_prev else made
@@ -227,26 +192,24 @@
     keep_rows = (rows_global < order // 2) == (rows_global < split_index[0])
     diag = (rows_global[:, None] == start + jnp.arange(width, dtype=jnp.int32)[None, :]).astype(F32)
 
-    raw = {}
+    raw, shift = {}, offset
     for da, db in REL:
         j = at(GRID, da, db)
-        got = flip(lax.dynamic_slice(matrix, ((1 - core) * half + j * BLK, offset), (BLK, width)), "core")
-        kept = lax.dynamic_slice(matrix, (core * half + j * BLK, offset), (BLK, width))
+        give = lax.dynamic_slice(matrix, ((1 - core) * half + j * BLK, shift), (BLK, width))
+        if not raw:
+            give, shift = lax.optimization_barrier((give, offset))
+        got = flip(give, "core")
+        kept = lax.dynamic_slice(matrix, (core * half + j * BLK, offset if not raw else shift), (BLK, width))
         raw[da, db] = jnp.where(owner // 2 == chip, jnp.where(owner % 2 == core, kept, got), F32(0.0))
     block = scatter_sum(lambda da, db: raw[da, db], GRID)
     block = lax.dot_general(
-        block, factor_inverse, (((1,), (1,)), ((), ())), precision=lax.Precision.HIGHEST, preferred_element_type=F32
+        block, factor_inverse, (((1,), (1,)), ((), ())), precision=lax.Precision.HIGH, preferred_element_type=F32
     )
 
     me = jnp.stack([x, zh, y, zl, core]).astype(jnp.int32)
     own = [(d, got, flip(got, "core")) for d, got in spread(block, GRID)]
 
-    def both(part):
-        return [v for _, p, q in part for v in (p, q)], [d for d, _, _ in part]
-
-    partial = gram_part(me, matrix, *both(own[:4]))
-    partial = gram_part(me, matrix, *both(own[4:7]), partial)
-    pieces = gram_last(me, matrix, *both(own[7:]), partial)
+    pieces = gram(me, matrix, [v for _, p, q in own for v in (p, q)], [d for d, _, _ in own])
     parts = dict(zip(REL, pieces))
     block = scatter_sum(lambda da, db: parts[da, db], ROW) / order + inv_rows
 

time: 242 us -> 247 us (1.021)
  waiting for transfers between devices: 99.4 us -> 108 us
  Pallas kernels: 40 us -> 33.1 us
  starting transfers between devices: 72.8 us -> 77.1 us
    ppermute x36, waiting for transfers between devices: 64.4 us -> 72.5 us  [ring(): return lax.ppermute(v, axes[0], [(i, (i + by) % 4) for i in range(4)])]
    pallas_call x3 -> x1, Pallas kernels: 20.3 us -> 13.4 us  [gram(): pl.pallas_call(functools.partial(gram_kernel, dists, pair), out_shape=tup...]
    ppermute x36, starting transfers between devices: 52.3 us -> 55.2 us  [ring(): return lax.ppermute(v, axes[0], [(i, (i + by) % 4) for i in range(4)])]
  transfers between devices with their start and end apart: 66 -> 66, of which waited for: 31 -> 33; matrix products, arithmetic and copies ran while one was open for 6% -> 4% of each run, Pallas kernels for 12% -> 6%
where the time goes in v1:
time: 247 us; the launch traced here: 246 us
  waiting for transfers between devices  108 us (44%)
  starting transfers between devices  77.1 us (31%)
  Pallas kernels  33.1 us (13%)
  other arithmetic  16.3 us (7%)
  local copies, waits for them, and re-layouts  7.53 us (3%)
    ppermute x36, waiting for transfers between devices, ring(): return lax.ppermute(v, axes[0], [(i, (i + by) % 4) for i in range(4)])  72.5 us
    ppermute x36, starting transfers between devices, ring(): return lax.ppermute(v, axes[0], [(i, (i + by) % 4) for i in range(4)])  55.2 us
    ppermute x29, waiting for transfers between devices, flip(): return lax.ppermute(v, axis, [(0, 1), (1, 0)])  26.3 us
    ppermute x29, starting transfers between devices, flip(): return lax.ppermute(v, axis, [(0, 1), (1, 0)])  21.1 us
    pallas_call x3, Pallas kernels, product_part(): pl.pallas_call(functools.partial(product_kernel, n, int(prev is not None)...  19.8 us
    pallas_call x1, Pallas kernels, gram(): pl.pallas_call(functools.partial(gram_kernel, dists, pair), out_shape=tup...  13.4 us
    ppermute x1, waiting for transfers between devices, turn(): return lax.ppermute(v, ALL, perm)  9.02 us
  transfers between devices with their start and end apart: 66, of which 33 were waited for; matrix products, arithmetic and copies ran while one was open for 4% of the time, Pallas kernels for 6%

profile of v1, /device:TPU:0, one launch (start us, length us, event | category | flops | bytes accessed | tf_op | source)
XLA Modules:
  0.0 245.8 jit_solution(1555720236619685208)
XLA Ops:
  12.9 5.6 %collective-permute-done.6 = f32[64,512]{1,0:T(8,128)S(1)} collective-permute-done((f32[64,512]{1,0:T(8,128)S(1)}, f32[64,512]{1,0:T(8,128)S(1)}, u32[]{:S(2)}, u32[]{:S(2)}) %collective-permute-start.6) | collective-permute-done | bytes 131104 | tf_op jit(solution)/shard_map/ppermute | solution.py:120
  25.9 3.3 %collective-permute-start.2 = (f32[128,512]{1,0:T(8,128)S(1)}, f32[128,512]{1,0:T(8,128)S(1)}, u32[]{:S(2)}, u32[]{:S(2)}) collective-permute-start(f32[128,512]{1,0:T(8,128)S(1)} %get-tuple-element.33), channel_id=1, source_target_pairs={{0,12},{4,0},{8,4},{12,8},{1,13},{5,1},{9,5},{13,9},{2,14},{6,2},{... | collective-permute-start | bytes 786440 | tf_op jit(solution)/shard_map/ppermute | solution.py:120
  37.0 7.8 %collective-permute-done.10 = f32[128,512]{1,0:T(8,128)S(1)} collective-permute-done((f32[128,512]{1,0:T(8,128)S(1)}, f32[128,512]{1,0:T(8,128)S(1)}, u32[]{:S(2)}, u32[]{:S(2)}) %collective-permute-start.10) | collective-permute-done | bytes 262176 | tf_op jit(solution)/shard_map/ppermute | solution.py:120
  48.7 4.2 %collective-permute-done.21.refs_8_ = f32[128,512]{1,0:T(8,128)S(1)} collective-permute-done((f32[128,512]{1,0:T(8,128)S(1)}, f32[128,512]{1,0:T(8,128)S(1)}, u32[]{:S(2)}, u32[]{:S(2)}) %collective-permute-start.21) | collective-permute-done | bytes 262176 | tf_op jit(solution)/shard_map/ppermute | solution.py:124
  54.9 8.4 %collective-permute-done.23.refs_10_ = f32[128,512]{1,0:T(8,128)S(1)} collective-permute-done((f32[128,512]{1,0:T(8,128)S(1)}, f32[128,512]{1,0:T(8,128)S(1)}, u32[]{:S(2)}, u32[]{:S(2)}) %collective-permute-start.23) | collective-permute-done | bytes 262176 | tf_op jit(solution)/shard_map/ppermute | solution.py:120
  69.6 6.1 %collective-permute-done.30 = f32[64,512]{1,0:T(8,128)S(1)} collective-permute-done((f32[64,512]{1,0:T(8,128)S(1)}, f32[64,512]{1,0:T(8,128)S(1)}, u32[]{:S(2)}, u32[]{:S(2)}) %collective-permute-start.30) | collective-permute-done | bytes 131104 | tf_op jit(solution)/shard_map/ppermute | solution.py:120
  79.6 13.4 %shard_map.46 = (f32[128,512]{1,0:T(8,128)}, f32[128,512]{1,0:T(8,128)}, f32[128,512]{1,0:T(8,128)}, f32[128,512]{1,0:T(8,128)}, f32[128,512]{1,0:T(8,128)}, /*i...) custom-call(s32[5]{0:T(128)} %stack.23.me, f32[2048,1024]{1,0:T(8,128)} %refs_3_.5, f32[2048,1024]{1,0:T(8,128)} %refs_3_.5, ...), custom_call_target="tpu_custom_call" | custom-call | tf_op jit(solution)/shard_map/pallas_call | solution.py:67
  102.7 3.7 %collective-permute-start.34 = (f32[128,512]{1,0:T(8,128)S(1)}, f32[128,512]{1,0:T(8,128)S(1)}, u32[]{:S(2)}, u32[]{:S(2)}) collective-permute-start(f32[128,512]{1,0:T(8,128)S(1)} %pad_add_fusion.3), channel_id=1, source_target_pairs={{0,16},{16,0},{1,17},{17,1},{2,18},{18,2},{3,19},{19,3},{4,20},{20... | collective-permute-start | bytes 786440 | tf_op jit(solution)/shard_map/ppermute | solution.py:124
  113.1 3.5 %collective-permute-done.38 = f32[128,512]{1,0:T(8,128)S(1)} collective-permute-done((f32[128,512]{1,0:T(8,128)S(1)}, f32[128,512]{1,0:T(8,128)S(1)}, u32[]{:S(2)}, u32[]{:S(2)}) %collective-permute-start.38) | collective-permute-done | bytes 262176 | tf_op jit(solution)/shard_map/ppermute | solution.py:120
  120.6 5.3 %collective-permute-done.39 = f32[128,512]{1,0:T(8,128)S(1)} collective-permute-done((f32[128,512]{1,0:T(8,128)S(1)}, f32[128,512]{1,0:T(8,128)S(1)}, u32[]{:S(2)}, u32[]{:S(2)}) %collective-permute-start.39) | collective-permute-done | bytes 262176 | tf_op jit(solution)/shard_map/ppermute | solution.py:124
  129.0 7.6 %collective-permute-done.40.refs_7_ = f32[128,512]{1,0:T(8,128)S(1)} collective-permute-done((f32[128,512]{1,0:T(8,128)S(1)}, f32[128,512]{1,0:T(8,128)S(1)}, u32[]{:S(2)}, u32[]{:S(2)}) %collective-permute-start.40) | collective-permute-done | bytes 262176 | tf_op jit(solution)/shard_map/ppermute | solution.py:124
  138.9 3.7 %collective-permute-start.43 = (f32[128,512]{1,0:T(8,128)S(1)}, f32[128,512]{1,0:T(8,128)S(1)}, u32[]{:S(2)}, u32[]{:S(2)}) collective-permute-start(f32[128,512]{1,0:T(8,128)S(1)} %collective-permute-done.42.refs_6_), channel_id=1, source_target_pairs={{0,96},{32,0},{64,32},{96,64},{1,97},{33,1},{65,33},{97,65},{2,98}... | collective-permute-start | bytes 786440 | tf_op jit(solution)/shard_map/ppermute | solution.py:120
  148.6 8.2 %shard_map.47.refs_8_ = f32[2048,512]{1,0:T(8,128)} custom-call(s32[5]{0:T(128)} %stack.23.me, f32[2048,1024]{1,0:T(8,128)} %refs_3_.5, f32[2048,1024]{1,0:T(8,128)} %refs_3_.5, f32[2048,1024]{1,0:T(8,128)} %refs_3_.5, f32[2048,1024]{1,0:T(8,128)} %refs_3_.5, f32[128,512]{1,0:T(8,128)} %copy-done.7, f32[128,512]{1,0:T(8,128)} %copy-done.20, ...), custom_call_target="tpu_custom_call" | custom-call | flops 3221225472 | bytes 8388608 | tf_op jit(solution)/shard_map/pallas_call | solution.py:103
  158.3 5.8 %shard_map.49 = f32[1024,512]{1,0:T(8,128)} custom-call(s32[5]{0:T(128)} %stack.23.me, f32[2048,1024]{1,0:T(8,128)} %refs_3_.5, f32[2048,1024]{1,0:T(8,128)} %refs_3_.5, f32[2048,1024]{1,0:T(8,128)} %refs_3_.5, f32[2048,1024]{1,0:T(8,128)} %refs_3_.5, f32[128,512]{1,0:T(8,128)} %copy-done.2, f32[128,512]{1,0:T(8,128)} %copy-done.5, f32[128,512]{1,0:T(8,128)} %copy-done.3, ...), custom_call_target="tpu_custom_call" | custom-call | flops 1610612736 | bytes 4194304 | tf_op jit(solution)/shard_map/pallas_call | solution.py:103
  164.1 5.8 %shard_map.48 = f32[1024,512]{1,0:T(8,128)} custom-call(s32[5]{0:T(128)} %stack.23.me, f32[2048,1024]{1,0:T(8,128)} %refs_3_.5, f32[2048,1024]{1,0:T(8,128)} %refs_3_.5, f32[2048,1024]{1,0:T(8,128)} %refs_3_.5, f32[2048,1024]{1,0:T(8,128)} %refs_3_.5, f32[128,512]{1,0:T(8,128)} %copy-done.2, f32[128,512]{1,0:T(8,128)} %copy-done.5, f32[128,512]{1,0:T(8,128)} %copy-done.3, ...), custom_call_target="tpu_custom_call" | custom-call | flops 1610612736 | bytes 4194304 | tf_op jit(solution)/shard_map/pallas_call | solution.py:103
  171.2 3.7 %collective-permute-start.54 = (f32[64,512]{1,0:T(8,128)S(1)}, f32[64,512]{1,0:T(8,128)}, u32[]{:S(2)}, u32[]{:S(2)}) collective-permute-start(f32[64,512]{1,0:T(8,128)S(1)} %get-tuple-element.46), channel_id=1, source_target_pairs={{0,12},{4,0},{8,4},{12,8},{1,13},{5,1},{9,5},{13,9},{2,14},{6,2},{... | collective-permute-start | bytes 393224 | tf_op jit(solution)/shard_map/ppermute | solution.py:120
  174.8 4.1 %collective-permute-done.50 = f32[64,512]{1,0:T(8,128)S(1)} collective-permute-done((f32[64,512]{1,0:T(8,128)S(1)}, f32[64,512]{1,0:T(8,128)S(1)}, u32[]{:S(2)}, u32[]{:S(2)}) %collective-permute-start.50) | collective-permute-done | bytes 131104 | tf_op jit(solution)/shard_map/ppermute | solution.py:120
  186.3 3.3 %collective-permute-done.51 = f32[128,512]{1,0:T(8,128)} collective-permute-done((f32[128,512]{1,0:T(8,128)}, f32[128,512]{1,0:T(8,128)}, u32[]{:S(2)}, u32[]{:S(2)}) %collective-permute-start.51) | collective-permute-done | bytes 262176 | tf_op jit(solution)/shard_map/ppermute | solution.py:124
  198.6 3.4 %collective-permute-done.53 = f32[128,512]{1,0:T(8,128)} collective-permute-done((f32[128,512]{1,0:T(8,128)}, f32[128,512]{1,0:T(8,128)}, u32[]{:S(2)}, u32[]{:S(2)}) %collective-permute-start.53) | collective-permute-done | bytes 262176 | tf_op jit(solution)/shard_map/ppermute | solution.py:120
  204.6 9.0 %collective-permute-done.57 = f32[128,512]{1,0:T(8,128)S(1)} collective-permute-done((f32[128,512]{1,0:T(8,128)S(1)}, f32[128,512]{1,0:T(8,128)S(1)}, u32[]{:S(2)}, u32[]{:S(2)}) %collective-permute-start.57) | collective-permute-done | bytes 262176 | tf_op jit(solution)/shard_map/ppermute | solution.py:171
  213.7 5.2 %collective-permute-start.59 = (f32[128,512]{1,0:T(8,128)S(1)}, f32[128,512]{1,0:T(8,128)S(1)}, u32[]{:S(2)}, u32[]{:S(2)}) collective-permute-start(f32[128,512]{1,0:T(8,128)S(1)} %collective-permute-done.57), channel_id=1, source_target_pairs={{0,96},{32,0},{64,32},{96,64},{1,97},{33,1},{65,33},{97,65},{2,98}... | collective-permute-start | bytes 786440 | tf_op jit(solution)/shard_map/ppermute | solution.py:120
  223.7 3.7 %collective-permute-start.62 = (f32[128,512]{1,0:T(8,128)S(1)}, f32[128,512]{1,0:T(8,128)S(1)}, u32[]{:S(2)}, u32[]{:S(2)}) collective-permute-start(f32[128,512]{1,0:T(8,128)S(1)} %collective-permute-done.59), channel_id=1, source_target_pairs={{0,96},{32,0},{64,32},{96,64},{1,97},{33,1},{65,33},{97,65},{2,98}... | collective-permute-start | bytes 786440 | tf_op jit(solution)/shard_map/ppermute | solution.py:120
  230.4 8.3 %collective-permute-done.61 = f32[128,512]{1,0:T(8,128)S(1)} collective-permute-done((f32[128,512]{1,0:T(8,128)S(1)}, f32[128,512]{1,0:T(8,128)S(1)}, u32[]{:S(2)}, u32[]{:S(2)}) %collective-permute-start.61) | collective-permute-done | bytes 262176 | tf_op jit(solution)/shard_map/ppermute | solution.py:120
  238.9 3.3 %collective-permute-start.65 = (f32[64,512]{1,0:T(8,128)S(1)}, f32[64,512]{1,0:T(8,128)S(1)}, u32[]{:S(2)}, u32[]{:S(2)}) collective-permute-start(f32[64,512]{1,0:T(8,128)S(1)} %slice.57), channel_id=1, source_target_pairs={{0,96},{32,0},{64,32},{96,64},{1,97},{33,1},{65,33},{97,65},{2,98}... | collective-permute-start | bytes 393224 | tf_op jit(solution)/shard_map/ppermute | solution.py:120
  (204 shorter events, 107.3 us)
Async XLA Ops:
  8.8 10.3 %collective-permute-start.1 = (f32[128,512]{1,0:T(8,128)S(1)}, f32[128,512]{1,0:T(8,128)S(1)}, u32[]{:S(2)}, u32[]{:S(2)}) collective-permute-start(f32[128,512]{1,0:T(8,128)S(1)} %get-tuple-element.32), channel_id=1, source_target_pairs={{0,1},{1,0},{2,3},{3,2},{4,5},{5,4},{6,7},{7,6},{8,9},{9,8},{10,11... | collective-permute-start | bytes 786440 | tf_op jit(solution)/shard_map/ppermute | solution.py:124
  8.8 10.9 %collective-permute-start.12 = (f32[128,512]{1,0:T(8,128)S(1)}, f32[128,512]{1,0:T(8,128)}, u32[]{:S(2)}, u32[]{:S(2)}) collective-permute-start(f32[128,512]{1,0:T(8,128)S(1)} %get-tuple-element.26), channel_id=1, source_target_pairs={{0,1},{1,0},{2,3},{3,2},{4,5},{5,4},{6,7},{7,6},{8,9},{9,8},{10,11... | collective-permute-start | bytes 786440 | tf_op jit(solution)/shard_map/ppermute | solution.py:124
  9.3 10.3 %collective-permute-start.4 = (f32[128,512]{1,0:T(8,128)S(1)}, f32[128,512]{1,0:T(8,128)}, u32[]{:S(2)}, u32[]{:S(2)}) collective-permute-start(f32[128,512]{1,0:T(8,128)S(1)} %get-tuple-element.30), channel_id=1, source_target_pairs={{0,1},{1,0},{2,3},{3,2},{4,5},{5,4},{6,7},{7,6},{8,9},{9,8},{10,11... | collective-permute-start | bytes 786440 | tf_op jit(solution)/shard_map/ppermute | solution.py:124
  9.3 10.5 %collective-permute-start.8 = (f32[128,512]{1,0:T(8,128)S(1)}, f32[128,512]{1,0:T(8,128)}, u32[]{:S(2)}, u32[]{:S(2)}) collective-permute-start(f32[128,512]{1,0:T(8,128)S(1)} %get-tuple-element.28), channel_id=1, source_target_pairs={{0,1},{1,0},{2,3},{3,2},{4,5},{5,4},{6,7},{7,6},{8,9},{9,8},{10,11... | collective-permute-start | bytes 786440 | tf_op jit(solution)/shard_map/ppermute | solution.py:124
  25.9 11.1 %collective-permute-start = (f32[128,512]{1,0:T(8,128)S(1)}, f32[128,512]{1,0:T(8,128)S(1)}, u32[]{:S(2)}, u32[]{:S(2)}) collective-permute-start(f32[128,512]{1,0:T(8,128)S(1)} %get-tuple-element.25), channel_id=1, source_target_pairs={{0,1},{1,0},{2,3},{3,2},{4,5},{5,4},{6,7},{7,6},{8,9},{9,8},{10,11... | collective-permute-start | bytes 786440 | tf_op jit(solution)/shard_map/ppermute | solution.py:124
  25.9 11.1 %collective-permute-start.2 = (f32[128,512]{1,0:T(8,128)S(1)}, f32[128,512]{1,0:T(8,128)S(1)}, u32[]{:S(2)}, u32[]{:S(2)}) collective-permute-start(f32[128,512]{1,0:T(8,128)S(1)} %get-tuple-element.33), channel_id=1, source_target_pairs={{0,12},{4,0},{8,4},{12,8},{1,13},{5,1},{9,5},{13,9},{2,14},{6,2},{... | collective-permute-start | bytes 786440 | tf_op jit(solution)/shard_map/ppermute | solution.py:120
  52.9 10.4 %collective-permute-start.23 = (f32[128,512]{1,0:T(8,128)S(1)}, f32[128,512]{1,0:T(8,128)S(1)}, u32[]{:S(2)}, u32[]{:S(2)}) collective-permute-start(f32[128,512]{1,0:T(8,128)S(1)} %collective-permute-done.21.refs_8_), channel_id=1, source_target_pairs={{0,4},{4,8},{8,12},{12,0},{1,5},{5,9},{9,13},{13,1},{2,6},{6,10},{... | collective-permute-start | bytes 786440 | tf_op jit(solution)/shard_map/ppermute | solution.py:120
  52.9 13.7 %collective-permute-start.17 = (f32[128,512]{1,0:T(8,128)S(1)}, f32[128,512]{1,0:T(8,128)S(1)}, u32[]{:S(2)}, u32[]{:S(2)}) collective-permute-start(f32[128,512]{1,0:T(8,128)S(1)} %fusion.refs_2_), channel_id=1, source_target_pairs={{0,4},{4,8},{8,12},{12,0},{1,5},{5,9},{9,13},{13,1},{2,6},{6,10},{... | collective-permute-start | bytes 786440 | tf_op jit(solution)/shard_map/ppermute | solution.py:120
  53.4 13.5 %collective-permute-start.27 = (f32[128,512]{1,0:T(8,128)S(1)}, f32[128,512]{1,0:T(8,128)S(1)}, u32[]{:S(2)}, u32[]{:S(2)}) collective-permute-start(f32[128,512]{1,0:T(8,128)S(1)} %collective-permute-done.19.refs_6_), channel_id=1, source_target_pairs={{0,2},{2,0},{1,3},{3,1},{4,6},{6,4},{5,7},{7,5},{8,10},{10,8},{9,1... | collective-permute-start | bytes 786440 | tf_op jit(solution)/shard_map/ppermute | solution.py:124
  63.4 12.3 %collective-permute-start.16 = (f32[128,512]{1,0:T(8,128)S(1)}, f32[128,512]{1,0:T(8,128)S(1)}, u32[]{:S(2)}, u32[]{:S(2)}) collective-permute-start(f32[128,512]{1,0:T(8,128)S(1)} %fusion.refs_2_), channel_id=1, source_target_pairs={{0,1},{1,0},{2,3},{3,2},{4,5},{5,4},{6,7},{7,6},{8,9},{9,8},{10,11... | collective-permute-start | bytes 786440 | tf_op jit(solution)/shard_map/ppermute | solution.py:124
  63.5 12.8 %collective-permute-start.25 = (f32[128,512]{1,0:T(8,128)S(1)}, f32[128,512]{1,0:T(8,128)S(1)}, u32[]{:S(2)}, u32[]{:S(2)}) collective-permute-start(f32[128,512]{1,0:T(8,128)S(1)} %collective-permute-done.19.refs_6_), channel_id=1, source_target_pairs={{0,12},{4,0},{8,4},{12,8},{1,13},{5,1},{9,5},{13,9},{2,14},{6,2},{... | collective-permute-start | bytes 786440 | tf_op jit(solution)/shard_map/ppermute | solution.py:120
  66.9 10.0 %collective-permute-start.20 = (f32[128,512]{1,0:T(8,128)S(1)}, f32[128,512]{1,0:T(8,128)S(1)}, u32[]{:S(2)}, u32[]{:S(2)}) collective-permute-start(f32[128,512]{1,0:T(8,128)S(1)} %collective-permute-done.19.refs_6_), channel_id=1, source_target_pairs={{0,1},{1,0},{2,3},{3,2},{4,5},{5,4},{6,7},{7,6},{8,9},{9,8},{10,11... | collective-permute-start | bytes 786440 | tf_op jit(solution)/shard_map/ppermute | solution.py:124
  95.6 14.2 %collective-permute-start.35 = (f32[128,512]{1,0:T(8,128)}, f32[128,512]{1,0:T(8,128)S(1)}, u32[]{:S(2)}, u32[]{:S(2)}) collective-permute-start(f32[128,512]{1,0:T(8,128)} %get-tuple-element.22), channel_id=1, source_target_pairs={{0,32},{32,64},{64,96},{96,0},{1,33},{33,65},{65,97},{97,1},{2,34}... | collective-permute-start | bytes 786440 | tf_op jit(solution)/shard_map/ppermute | solution.py:120
  109.0 10.9 %collective-permute-start.32 = (f32[128,512]{1,0:T(8,128)}, f32[128,512]{1,0:T(8,128)S(1)}, u32[]{:S(2)}, u32[]{:S(2)}) collective-permute-start(f32[128,512]{1,0:T(8,128)} %get-tuple-element.18), channel_id=1, source_target_pairs={{0,96},{32,0},{64,32},{96,64},{1,97},{33,1},{65,33},{97,65},{2,98}... | collective-permute-start | bytes 786440 | tf_op jit(solution)/shard_map/ppermute | solution.py:120
  126.1 10.6 %collective-permute-start.40 = (f32[128,512]{1,0:T(8,128)S(1)}, f32[128,512]{1,0:T(8,128)S(1)}, u32[]{:S(2)}, u32[]{:S(2)}) collective-permute-start(f32[128,512]{1,0:T(8,128)S(1)} %bitcast_add_fusion.refs_4_), channel_id=1, source_target_pairs={{0,16},{16,0},{1,17},{17,1},{2,18},{18,2},{3,19},{19,3},{4,20},{20... | collective-permute-start | bytes 786440 | tf_op jit(solution)/shard_map/ppermute | solution.py:124
  126.2 10.5 %collective-permute-start.42 = (f32[128,512]{1,0:T(8,128)S(1)}, f32[128,512]{1,0:T(8,128)S(1)}, u32[]{:S(2)}, u32[]{:S(2)}) collective-permute-start(f32[128,512]{1,0:T(8,128)S(1)} %bitcast_add_fusion.refs_4_), channel_id=1, source_target_pairs={{0,96},{32,0},{64,32},{96,64},{1,97},{33,1},{65,33},{97,65},{2,98}... | collective-permute-start | bytes 786440 | tf_op jit(solution)/shard_map/ppermute | solution.py:120
  138.9 17.9 %collective-permute-start.43 = (f32[128,512]{1,0:T(8,128)S(1)}, f32[128,512]{1,0:T(8,128)S(1)}, u32[]{:S(2)}, u32[]{:S(2)}) collective-permute-start(f32[128,512]{1,0:T(8,128)S(1)} %collective-permute-done.42.refs_6_), channel_id=1, source_target_pairs={{0,96},{32,0},{64,32},{96,64},{1,97},{33,1},{65,33},{97,65},{2,98}... | collective-permute-start | bytes 786440 | tf_op jit(solution)/shard_map/ppermute | solution.py:120
  144.2 12.6 %collective-permute-start.45 = (f32[64,512]{1,0:T(8,128)S(1)}, f32[64,512]{1,0:T(8,128)S(1)}, u32[]{:S(2)}, u32[]{:S(2)}) collective-permute-start(f32[64,512]{1,0:T(8,128)S(1)} %slice.52), channel_id=1, source_target_pairs={{0,32},{32,64},{64,96},{96,0},{1,33},{33,65},{65,97},{97,1},{2,34}... | collective-permute-start | bytes 393224 | tf_op jit(solution)/shard_map/ppermute | solution.py:120
  144.6 12.2 %collective-permute-start.46 = (f32[64,512]{1,0:T(8,128)S(1)}, f32[64,512]{1,0:T(8,128)S(1)}, u32[]{:S(2)}, u32[]{:S(2)}) collective-permute-start(f32[64,512]{1,0:T(8,128)S(1)} %slice.53), channel_id=1, source_target_pairs={{0,96},{32,0},{64,32},{96,64},{1,97},{33,1},{65,33},{97,65},{2,98}... | collective-permute-start | bytes 393224 | tf_op jit(solution)/shard_map/ppermute | solution.py:120
  184.4 14.2 %collective-permute-start.49 = (f32[128,512]{1,0:T(8,128)S(1)}, f32[128,512]{1,0:T(8,128)}, u32[]{:S(2)}, u32[]{:S(2)}) collective-permute-start(f32[128,512]{1,0:T(8,128)S(1)} %get-tuple-element.39), channel_id=1, source_target_pairs={{0,12},{4,0},{8,4},{12,8},{1,13},{5,1},{9,5},{13,9},{2,14},{6,2},{... | collective-permute-start | bytes 786440 | tf_op jit(solution)/shard_map/ppermute | solution.py:120
  213.7 10.0 %collective-permute-start.59 = (f32[128,512]{1,0:T(8,128)S(1)}, f32[128,512]{1,0:T(8,128)S(1)}, u32[]{:S(2)}, u32[]{:S(2)}) collective-permute-start(f32[128,512]{1,0:T(8,128)S(1)} %collective-permute-done.57), channel_id=1, source_target_pairs={{0,96},{32,0},{64,32},{96,64},{1,97},{33,1},{65,33},{97,65},{2,98}... | collective-permute-start | bytes 786440 | tf_op jit(solution)/shard_map/ppermute | solution.py:120
  218.9 10.9 %collective-permute-start.60 = (f32[128,512]{1,0:T(8,128)S(1)}, f32[128,512]{1,0:T(8,128)S(1)}, u32[]{:S(2)}, u32[]{:S(2)}) collective-permute-start(f32[128,512]{1,0:T(8,128)S(1)} %collective-permute-done.57), channel_id=1, source_target_pairs={{0,16},{16,0},{1,17},{17,1},{2,18},{18,2},{3,19},{19,3},{4,20},{20... | collective-permute-start | bytes 786440 | tf_op jit(solution)/shard_map/ppermute | solution.py:124
  223.7 18.5 %collective-permute-start.62 = (f32[128,512]{1,0:T(8,128)S(1)}, f32[128,512]{1,0:T(8,128)S(1)}, u32[]{:S(2)}, u32[]{:S(2)}) collective-permute-start(f32[128,512]{1,0:T(8,128)S(1)} %collective-permute-done.59), channel_id=1, source_target_pairs={{0,96},{32,0},{64,32},{96,64},{1,97},{33,1},{65,33},{97,65},{2,98}... | collective-permute-start | bytes 786440 | tf_op jit(solution)/shard_map/ppermute | solution.py:120
  227.4 11.5 %collective-permute-start.63 = (f32[128,512]{1,0:T(8,128)S(1)}, f32[128,512]{1,0:T(8,128)S(1)}, u32[]{:S(2)}, u32[]{:S(2)}) collective-permute-start(f32[128,512]{1,0:T(8,128)S(1)} %collective-permute-done.59), channel_id=1, source_target_pairs={{0,16},{16,0},{1,17},{17,1},{2,18},{18,2},{3,19},{19,3},{4,20},{20... | collective-permute-start | bytes 786440 | tf_op jit(solution)/shard_map/ppermute | solution.py:124
  (67 other events, 608.4 us)

commit v2 on v1

--- a/solution.py
+++ b/solution.py
@@ -146,13 +146,14 @@
     far = blk(2, 1)
     n = far.shape[0] // 2
     u, w = ring(far[:n], axes, -1), ring(far[n:], axes, 1)
-    sp, tm = ring(blk(2, 0), axes, 1), ring(blk(3, 0), axes, -1)
+    held = lax.optimization_barrier({d: blk(*d) for d in REL[1:]})
+    sp, tm = ring(held[2, 0], axes, 1), ring(held[3, 0], axes, -1)
     none = jnp.zeros_like(u)
-    sz = flip(blk(1, 1) + jnp.concatenate([none, w], 0), axes[1])
-    sm = ring(blk(3, 1) + jnp.concatenate([u, none], 0), axes, -1)
-    tp = ring(blk(1, 0) + sz + sp, axes, 1)
-    tz = flip(blk(0, 1) + sm, axes[1])
-    return blk(0, 0) + tm + tp + tz
+    sz = flip(held[1, 1] + jnp.concatenate([none, w], 0), axes[1])
+    sm = ring(held[3, 1] + jnp.concatenate([u, none], 0), axes, -1)
+    tp = ring(held[1, 0] + sz + sp, axes, 1)
+    tz = flip(held[0, 1] + sm, axes[1])
+    return held[0, 0] + tm + tp + tz
 
 
 SPREAD_X = {0: 2, 1: 3, 3: 1, 2: 0}

time: 247 us -> 230 us (0.931)
  waiting for transfers between devices: 108 us -> 100 us
  starting transfers between devices: 77.1 us -> 73.3 us
  other arithmetic: 16.3 us -> 12.7 us
    ppermute x36, waiting for transfers between devices: 72.5 us -> 63.2 us  [ring(): return lax.ppermute(v, axes[0], [(i, (i + by) % 4) for i in range(4)])]
    ppermute x1, waiting for transfers between devices: 9.02 us -> 12.5 us  [turn(): return lax.ppermute(v, ALL, perm)]
    select_n x1 -> x2, other arithmetic: 1.97 us -> 4.65 us  [per_device(): jnp.where(owner // 2 == chip, jnp.where(owner % 2 == core, kept, got), F3...]
    add x6 -> x12, other arithmetic: 6.8 us -> 4.25 us  [the longest x3 2.08 us: scatter_sum(): tp = ring(held[1, 0] + sz + sp, axes, 1)]
  transfers between devices with their start and end apart: 66 -> 66, of which waited for: 33 -> 36; matrix products, arithmetic and copies ran while one was open for 4% -> 4% of each run, Pallas kernels for 6% -> 6%
where the time goes in v2:
time: 230 us; the launch traced here: 229 us
  waiting for transfers between devices  100 us (43%)
  starting transfers between devices  73.3 us (32%)
  Pallas kernels  33.1 us (14%)
  other arithmetic  12.7 us (6%)
  local copies, waits for them, and re-layouts  6.65 us (3%)
    ppermute x36, waiting for transfers between devices, ring(): return lax.ppermute(v, axes[0], [(i, (i + by) % 4) for i in range(4)])  63.2 us
    ppermute x36, starting transfers between devices, ring(): return lax.ppermute(v, axes[0], [(i, (i + by) % 4) for i in range(4)])  53.4 us
    ppermute x29, waiting for transfers between devices, flip(): return lax.ppermute(v, axis, [(0, 1), (1, 0)])  24.6 us
    pallas_call x3, Pallas kernels, product_part(): pl.pallas_call(functools.partial(product_kernel, n, int(prev is not None)...  19.7 us
    ppermute x29, starting transfers between devices, flip(): return lax.ppermute(v, axis, [(0, 1), (1, 0)])  19.2 us
    pallas_call x1, Pallas kernels, gram(): pl.pallas_call(functools.partial(gram_kernel, dists, pair), out_shape=tup...  13.4 us
    ppermute x1, waiting for transfers between devices, turn(): return lax.ppermute(v, ALL, perm)  12.5 us
    select_n x2, other arithmetic, per_device(): jnp.where(owner // 2 == chip, jnp.where(owner % 2 == core, kept, got), F3...  4.65 us
  transfers between devices with their start and end apart: 66, of which 36 were waited for; matrix products, arithmetic and copies ran while one was open for 4% of the time, Pallas kernels for 6%

profile of v2, /device:TPU:0, one launch (start us, length us, event | category | flops | bytes accessed | tf_op | source)
XLA Modules:
  0.0 229.0 jit_solution(31315494240046843)
XLA Ops:
  17.3 3.0 %collective-permute-start.14 = (f32[128,512]{1,0:T(8,128)S(1)}, f32[128,512]{1,0:T(8,128)S(1)}, u32[]{:S(2)}, u32[]{:S(2)}) collective-permute-start(f32[128,512]{1,0:T(8,128)S(1)} %pad_add_fusion.4), channel_id=1, source_target_pairs={{0,12},{4,0},{8,4},{12,8},{1,13},{5,1},{9,5},{13,9},{2,14},{6,2},{... | collective-permute-start | bytes 786440 | tf_op jit(solution)/shard_map/ppermute | solution.py:120
  27.3 3.3 %collective-permute-done.7 = f32[128,512]{1,0:T(8,128)S(1)} collective-permute-done((f32[128,512]{1,0:T(8,128)S(1)}, f32[128,512]{1,0:T(8,128)S(1)}, u32[]{:S(2)}, u32[]{:S(2)}) %collective-permute-start.7) | collective-permute-done | bytes 262176 | tf_op jit(solution)/shard_map/ppermute | solution.py:120
  30.6 2.9 %collective-permute-done.12 = f32[128,512]{1,0:T(8,128)S(1)} collective-permute-done((f32[128,512]{1,0:T(8,128)S(1)}, f32[128,512]{1,0:T(8,128)S(1)}, u32[]{:S(2)}, u32[]{:S(2)}) %collective-permute-start.12) | collective-permute-done | bytes 262176 | tf_op jit(solution)/shard_map/ppermute | solution.py:120
  34.9 4.5 %collective-permute-start.19 = (f32[128,512]{1,0:T(8,128)S(1)}, f32[128,512]{1,0:T(8,128)S(1)}, u32[]{:S(2)}, u32[]{:S(2)}) collective-permute-start(f32[128,512]{1,0:T(8,128)S(1)} %fusion.refs_2_), channel_id=1, source_target_pairs={{0,12},{4,0},{8,4},{12,8},{1,13},{5,1},{9,5},{13,9},{2,14},{6,2},{... | collective-permute-start | bytes 786440 | tf_op jit(solution)/shard_map/ppermute | solution.py:120
  45.2 7.5 %collective-permute-done.23.refs_10_ = f32[128,512]{1,0:T(8,128)S(1)} collective-permute-done((f32[128,512]{1,0:T(8,128)S(1)}, f32[128,512]{1,0:T(8,128)S(1)}, u32[]{:S(2)}, u32[]{:S(2)}) %collective-permute-start.23) | collective-permute-done | bytes 262176 | tf_op jit(solution)/shard_map/ppermute | solution.py:120
  52.9 3.1 %collective-permute-start.25 = (f32[128,512]{1,0:T(8,128)S(1)}, f32[128,512]{1,0:T(8,128)S(1)}, u32[]{:S(2)}, u32[]{:S(2)}) collective-permute-start(f32[128,512]{1,0:T(8,128)S(1)} %collective-permute-done.19.refs_6_), channel_id=1, source_target_pairs={{0,12},{4,0},{8,4},{12,8},{1,13},{5,1},{9,5},{13,9},{2,14},{6,2},{... | collective-permute-start | bytes 786440 | tf_op jit(solution)/shard_map/ppermute | solution.py:120
  59.8 5.3 %collective-permute-done.30 = f32[64,512]{1,0:T(8,128)S(1)} collective-permute-done((f32[64,512]{1,0:T(8,128)S(1)}, f32[64,512]{1,0:T(8,128)S(1)}, u32[]{:S(2)}, u32[]{:S(2)}) %collective-permute-start.30) | collective-permute-done | bytes 131104 | tf_op jit(solution)/shard_map/ppermute | solution.py:120
  69.1 13.4 %shard_map.46 = (f32[128,512]{1,0:T(8,128)}, f32[128,512]{1,0:T(8,128)}, f32[128,512]{1,0:T(8,128)}, f32[128,512]{1,0:T(8,128)}, f32[128,512]{1,0:T(8,128)}, /*i...) custom-call(s32[5]{0:T(128)} %stack.23.me, f32[2048,1024]{1,0:T(8,128)} %refs_3_.5, f32[2048,1024]{1,0:T(8,128)} %refs_3_.5, ...), custom_call_target="tpu_custom_call" | custom-call | tf_op jit(solution)/shard_map/pallas_call | solution.py:67
  88.3 2.9 %collective-permute-done.33 = f32[64,512]{1,0:T(8,128)S(1)} collective-permute-done((f32[64,512]{1,0:T(8,128)S(1)}, f32[64,512]{1,0:T(8,128)S(1)}, u32[]{:S(2)}, u32[]{:S(2)}) %collective-permute-start.33) | collective-permute-done | bytes 131104 | tf_op jit(solution)/shard_map/ppermute | solution.py:120
  92.1 3.5 %collective-permute-start.34 = (f32[128,512]{1,0:T(8,128)S(1)}, f32[128,512]{1,0:T(8,128)S(1)}, u32[]{:S(2)}, u32[]{:S(2)}) collective-permute-start(f32[128,512]{1,0:T(8,128)S(1)} %pad_add_fusion.3), channel_id=1, source_target_pairs={{0,16},{16,0},{1,17},{17,1},{2,18},{18,2},{3,19},{19,3},{4,20},{20... | collective-permute-start | bytes 786440 | tf_op jit(solution)/shard_map/ppermute | solution.py:124
  102.4 3.5 %collective-permute-done.38 = f32[128,512]{1,0:T(8,128)S(1)} collective-permute-done((f32[128,512]{1,0:T(8,128)S(1)}, f32[128,512]{1,0:T(8,128)S(1)}, u32[]{:S(2)}, u32[]{:S(2)}) %collective-permute-start.38) | collective-permute-done | bytes 262176 | tf_op jit(solution)/shard_map/ppermute | solution.py:120
  109.7 5.5 %collective-permute-done.39 = f32[128,512]{1,0:T(8,128)S(1)} collective-permute-done((f32[128,512]{1,0:T(8,128)S(1)}, f32[128,512]{1,0:T(8,128)S(1)}, u32[]{:S(2)}, u32[]{:S(2)}) %collective-permute-start.39) | collective-permute-done | bytes 262176 | tf_op jit(solution)/shard_map/ppermute | solution.py:124
  118.2 7.7 %collective-permute-done.40.refs_7_ = f32[128,512]{1,0:T(8,128)S(1)} collective-permute-done((f32[128,512]{1,0:T(8,128)S(1)}, f32[128,512]{1,0:T(8,128)S(1)}, u32[]{:S(2)}, u32[]{:S(2)}) %collective-permute-start.40) | collective-permute-done | bytes 262176 | tf_op jit(solution)/shard_map/ppermute | solution.py:124
  128.1 3.7 %collective-permute-start.43 = (f32[128,512]{1,0:T(8,128)S(1)}, f32[128,512]{1,0:T(8,128)S(1)}, u32[]{:S(2)}, u32[]{:S(2)}) collective-permute-start(f32[128,512]{1,0:T(8,128)S(1)} %collective-permute-done.42.refs_6_), channel_id=1, source_target_pairs={{0,96},{32,0},{64,32},{96,64},{1,97},{33,1},{65,33},{97,65},{2,98}... | collective-permute-start | bytes 786440 | tf_op jit(solution)/shard_map/ppermute | solution.py:120
  133.9 3.2 %collective-permute-start.46 = (f32[64,512]{1,0:T(8,128)S(1)}, f32[64,512]{1,0:T(8,128)S(1)}, u32[]{:S(2)}, u32[]{:S(2)}) collective-permute-start(f32[64,512]{1,0:T(8,128)S(1)} %slice.53), channel_id=1, source_target_pairs={{0,96},{32,0},{64,32},{96,64},{1,97},{33,1},{65,33},{97,65},{2,98}... | collective-permute-start | bytes 393224 | tf_op jit(solution)/shard_map/ppermute | solution.py:120
  137.9 8.2 %shard_map.47.refs_8_ = f32[2048,512]{1,0:T(8,128)} custom-call(s32[5]{0:T(128)} %stack.23.me, f32[2048,1024]{1,0:T(8,128)} %refs_3_.5, f32[2048,1024]{1,0:T(8,128)} %refs_3_.5, f32[2048,1024]{1,0:T(8,128)} %refs_3_.5, f32[2048,1024]{1,0:T(8,128)} %refs_3_.5, f32[128,512]{1,0:T(8,128)} %copy-done.7, f32[128,512]{1,0:T(8,128)} %copy-done.21, ...), custom_call_target="tpu_custom_call" | custom-call | flops 3221225472 | bytes 8388608 | tf_op jit(solution)/shard_map/pallas_call | solution.py:103
  147.6 5.8 %shard_map.49 = f32[1024,512]{1,0:T(8,128)} custom-call(s32[5]{0:T(128)} %stack.23.me, f32[2048,1024]{1,0:T(8,128)} %refs_3_.5, f32[2048,1024]{1,0:T(8,128)} %refs_3_.5, f32[2048,1024]{1,0:T(8,128)} %refs_3_.5, f32[2048,1024]{1,0:T(8,128)} %refs_3_.5, f32[128,512]{1,0:T(8,128)} %copy-done.2, f32[128,512]{1,0:T(8,128)} %copy-done.5, f32[128,512]{1,0:T(8,128)} %copy-done.3, ...), custom_call_target="tpu_custom_call" | custom-call | flops 1610612736 | bytes 4194304 | tf_op jit(solution)/shard_map/pallas_call | solution.py:103
  153.4 5.8 %shard_map.48 = f32[1024,512]{1,0:T(8,128)} custom-call(s32[5]{0:T(128)} %stack.23.me, f32[2048,1024]{1,0:T(8,128)} %refs_3_.5, f32[2048,1024]{1,0:T(8,128)} %refs_3_.5, f32[2048,1024]{1,0:T(8,128)} %refs_3_.5, f32[2048,1024]{1,0:T(8,128)} %refs_3_.5, f32[128,512]{1,0:T(8,128)} %copy-done.2, f32[128,512]{1,0:T(8,128)} %copy-done.5, f32[128,512]{1,0:T(8,128)} %copy-done.3, ...), custom_call_target="tpu_custom_call" | custom-call | flops 1610612736 | bytes 4194304 | tf_op jit(solution)/shard_map/pallas_call | solution.py:103
  166.3 3.8 %collective-permute-done.50 = f32[64,512]{1,0:T(8,128)S(1)} collective-permute-done((f32[64,512]{1,0:T(8,128)S(1)}, f32[64,512]{1,0:T(8,128)S(1)}, u32[]{:S(2)}, u32[]{:S(2)}) %collective-permute-start.50) | collective-permute-done | bytes 131104 | tf_op jit(solution)/shard_map/ppermute | solution.py:120
  184.0 3.4 %collective-permute-done.53 = f32[128,512]{1,0:T(8,128)S(1)} collective-permute-done((f32[128,512]{1,0:T(8,128)S(1)}, f32[128,512]{1,0:T(8,128)S(1)}, u32[]{:S(2)}, u32[]{:S(2)}) %collective-permute-start.53) | collective-permute-done | bytes 262176 | tf_op jit(solution)/shard_map/ppermute | solution.py:120
  188.2 12.5 %collective-permute-done.57 = f32[128,512]{1,0:T(8,128)S(1)} collective-permute-done((f32[128,512]{1,0:T(8,128)S(1)}, f32[128,512]{1,0:T(8,128)S(1)}, u32[]{:S(2)}, u32[]{:S(2)}) %collective-permute-start.57) | collective-permute-done | bytes 262176 | tf_op jit(solution)/shard_map/ppermute | solution.py:172
  206.6 3.0 %collective-permute-done.59 = f32[128,512]{1,0:T(8,128)S(1)} collective-permute-done((f32[128,512]{1,0:T(8,128)S(1)}, f32[128,512]{1,0:T(8,128)S(1)}, u32[]{:S(2)}, u32[]{:S(2)}) %collective-permute-start.59) | collective-permute-done | bytes 262176 | tf_op jit(solution)/shard_map/ppermute | solution.py:120
  214.4 7.6 %collective-permute-done.61 = f32[128,512]{1,0:T(8,128)S(1)} collective-permute-done((f32[128,512]{1,0:T(8,128)S(1)}, f32[128,512]{1,0:T(8,128)S(1)}, u32[]{:S(2)}, u32[]{:S(2)}) %collective-permute-start.61) | collective-permute-done | bytes 262176 | tf_op jit(solution)/shard_map/ppermute | solution.py:120
  222.2 3.3 %collective-permute-start.65 = (f32[64,512]{1,0:T(8,128)S(1)}, f32[64,512]{1,0:T(8,128)S(1)}, u32[]{:S(2)}, u32[]{:S(2)}) collective-permute-start(f32[64,512]{1,0:T(8,128)S(1)} %slice.57), channel_id=1, source_target_pairs={{0,96},{32,0},{64,32},{96,64},{1,97},{33,1},{65,33},{97,65},{2,98}... | collective-permute-start | bytes 393224 | tf_op jit(solution)/shard_map/ppermute | solution.py:120
  (207 shorter events, 100.6 us)
Async XLA Ops:
  17.3 9.7 %collective-permute-start.14 = (f32[128,512]{1,0:T(8,128)S(1)}, f32[128,512]{1,0:T(8,128)S(1)}, u32[]{:S(2)}, u32[]{:S(2)}) collective-permute-start(f32[128,512]{1,0:T(8,128)S(1)} %pad_add_fusion.4), channel_id=1, source_target_pairs={{0,12},{4,0},{8,4},{12,8},{1,13},{5,1},{9,5},{13,9},{2,14},{6,2},{... | collective-permute-start | bytes 786440 | tf_op jit(solution)/shard_map/ppermute | solution.py:120
  20.3 10.2 %collective-permute-start.7 = (f32[128,512]{1,0:T(8,128)S(1)}, f32[128,512]{1,0:T(8,128)S(1)}, u32[]{:S(2)}, u32[]{:S(2)}) collective-permute-start(f32[128,512]{1,0:T(8,128)S(1)} %get-tuple-element.38), channel_id=1, source_target_pairs={{0,12},{4,0},{8,4},{12,8},{1,13},{5,1},{9,5},{13,9},{2,14},{6,2},{... | collective-permute-start | bytes 786440 | tf_op jit(solution)/shard_map/ppermute | solution.py:120
  34.9 10.3 %collective-permute-start.19 = (f32[128,512]{1,0:T(8,128)S(1)}, f32[128,512]{1,0:T(8,128)S(1)}, u32[]{:S(2)}, u32[]{:S(2)}) collective-permute-start(f32[128,512]{1,0:T(8,128)S(1)} %fusion.refs_2_), channel_id=1, source_target_pairs={{0,12},{4,0},{8,4},{12,8},{1,13},{5,1},{9,5},{13,9},{2,14},{6,2},{... | collective-permute-start | bytes 786440 | tf_op jit(solution)/shard_map/ppermute | solution.py:120
  40.8 12.0 %collective-permute-start.23 = (f32[128,512]{1,0:T(8,128)S(1)}, f32[128,512]{1,0:T(8,128)S(1)}, u32[]{:S(2)}, u32[]{:S(2)}) collective-permute-start(f32[128,512]{1,0:T(8,128)S(1)} %collective-permute-done.21.refs_8_), channel_id=1, source_target_pairs={{0,4},{4,8},{8,12},{12,0},{1,5},{5,9},{9,13},{13,1},{2,6},{6,10},{... | collective-permute-start | bytes 786440 | tf_op jit(solution)/shard_map/ppermute | solution.py:120
  42.8 13.2 %collective-permute-start.17 = (f32[128,512]{1,0:T(8,128)S(1)}, f32[128,512]{1,0:T(8,128)S(1)}, u32[]{:S(2)}, u32[]{:S(2)}) collective-permute-start(f32[128,512]{1,0:T(8,128)S(1)} %fusion.refs_2_), channel_id=1, source_target_pairs={{0,4},{4,8},{8,12},{12,0},{1,5},{5,9},{9,13},{13,1},{2,6},{6,10},{... | collective-permute-start | bytes 786440 | tf_op jit(solution)/shard_map/ppermute | solution.py:120
  45.2 11.1 %collective-permute-start.27 = (f32[128,512]{1,0:T(8,128)S(1)}, f32[128,512]{1,0:T(8,128)S(1)}, u32[]{:S(2)}, u32[]{:S(2)}) collective-permute-start(f32[128,512]{1,0:T(8,128)S(1)} %collective-permute-done.19.refs_6_), channel_id=1, source_target_pairs={{0,2},{2,0},{1,3},{3,1},{4,6},{6,4},{5,7},{7,5},{8,10},{10,8},{9,1... | collective-permute-start | bytes 786440 | tf_op jit(solution)/shard_map/ppermute | solution.py:124
  52.8 12.3 %collective-permute-start.16 = (f32[128,512]{1,0:T(8,128)S(1)}, f32[128,512]{1,0:T(8,128)S(1)}, u32[]{:S(2)}, u32[]{:S(2)}) collective-permute-start(f32[128,512]{1,0:T(8,128)S(1)} %fusion.refs_2_), channel_id=1, source_target_pairs={{0,1},{1,0},{2,3},{3,2},{4,5},{5,4},{6,7},{7,6},{8,9},{9,8},{10,11... | collective-permute-start | bytes 786440 | tf_op jit(solution)/shard_map/ppermute | solution.py:124
  52.9 12.8 %collective-permute-start.25 = (f32[128,512]{1,0:T(8,128)S(1)}, f32[128,512]{1,0:T(8,128)S(1)}, u32[]{:S(2)}, u32[]{:S(2)}) collective-permute-start(f32[128,512]{1,0:T(8,128)S(1)} %collective-permute-done.19.refs_6_), channel_id=1, source_target_pairs={{0,12},{4,0},{8,4},{12,8},{1,13},{5,1},{9,5},{13,9},{2,14},{6,2},{... | collective-permute-start | bytes 786440 | tf_op jit(solution)/shard_map/ppermute | solution.py:120
  56.1 9.8 %collective-permute-start.18 = (f32[128,512]{1,0:T(8,128)S(1)}, f32[128,512]{1,0:T(8,128)S(1)}, u32[]{:S(2)}, u32[]{:S(2)}) collective-permute-start(f32[128,512]{1,0:T(8,128)S(1)} %collective-permute-done.17.refs_4_), channel_id=1, source_target_pairs={{0,1},{1,0},{2,3},{3,2},{4,5},{5,4},{6,7},{7,6},{8,9},{9,8},{10,11... | collective-permute-start | bytes 786440 | tf_op jit(solution)/shard_map/ppermute | solution.py:124
  56.3 10.0 %collective-permute-start.20 = (f32[128,512]{1,0:T(8,128)S(1)}, f32[128,512]{1,0:T(8,128)S(1)}, u32[]{:S(2)}, u32[]{:S(2)}) collective-permute-start(f32[128,512]{1,0:T(8,128)S(1)} %collective-permute-done.19.refs_6_), channel_id=1, source_target_pairs={{0,1},{1,0},{2,3},{3,2},{4,5},{5,4},{6,7},{7,6},{8,9},{9,8},{10,11... | collective-permute-start | bytes 786440 | tf_op jit(solution)/shard_map/ppermute | solution.py:124
  85.1 14.0 %collective-permute-start.35 = (f32[128,512]{1,0:T(8,128)}, f32[128,512]{1,0:T(8,128)S(1)}, u32[]{:S(2)}, u32[]{:S(2)}) collective-permute-start(f32[128,512]{1,0:T(8,128)} %get-tuple-element.57), channel_id=1, source_target_pairs={{0,32},{32,64},{64,96},{96,0},{1,33},{33,65},{65,97},{97,1},{2,34}... | collective-permute-start | bytes 786440 | tf_op jit(solution)/shard_map/ppermute | solution.py:120
  98.2 11.0 %collective-permute-start.32 = (f32[128,512]{1,0:T(8,128)}, f32[128,512]{1,0:T(8,128)S(1)}, u32[]{:S(2)}, u32[]{:S(2)}) collective-permute-start(f32[128,512]{1,0:T(8,128)} %get-tuple-element.53), channel_id=1, source_target_pairs={{0,96},{32,0},{64,32},{96,64},{1,97},{33,1},{65,33},{97,65},{2,98}... | collective-permute-start | bytes 786440 | tf_op jit(solution)/shard_map/ppermute | solution.py:120
  115.3 10.6 %collective-permute-start.40 = (f32[128,512]{1,0:T(8,128)S(1)}, f32[128,512]{1,0:T(8,128)S(1)}, u32[]{:S(2)}, u32[]{:S(2)}) collective-permute-start(f32[128,512]{1,0:T(8,128)S(1)} %bitcast_add_fusion.refs_4_), channel_id=1, source_target_pairs={{0,16},{16,0},{1,17},{17,1},{2,18},{18,2},{3,19},{19,3},{4,20},{20... | collective-permute-start | bytes 786440 | tf_op jit(solution)/shard_map/ppermute | solution.py:124
  115.4 10.5 %collective-permute-start.42 = (f32[128,512]{1,0:T(8,128)S(1)}, f32[128,512]{1,0:T(8,128)S(1)}, u32[]{:S(2)}, u32[]{:S(2)}) collective-permute-start(f32[128,512]{1,0:T(8,128)S(1)} %bitcast_add_fusion.refs_4_), channel_id=1, source_target_pairs={{0,96},{32,0},{64,32},{96,64},{1,97},{33,1},{65,33},{97,65},{2,98}... | collective-permute-start | bytes 786440 | tf_op jit(solution)/shard_map/ppermute | solution.py:120
  128.1 18.1 %collective-permute-start.43 = (f32[128,512]{1,0:T(8,128)S(1)}, f32[128,512]{1,0:T(8,128)S(1)}, u32[]{:S(2)}, u32[]{:S(2)}) collective-permute-start(f32[128,512]{1,0:T(8,128)S(1)} %collective-permute-done.42.refs_6_), channel_id=1, source_target_pairs={{0,96},{32,0},{64,32},{96,64},{1,97},{33,1},{65,33},{97,65},{2,98}... | collective-permute-start | bytes 786440 | tf_op jit(solution)/shard_map/ppermute | solution.py:120
  133.5 12.6 %collective-permute-start.45 = (f32[64,512]{1,0:T(8,128)S(1)}, f32[64,512]{1,0:T(8,128)S(1)}, u32[]{:S(2)}, u32[]{:S(2)}) collective-permute-start(f32[64,512]{1,0:T(8,128)S(1)} %slice.52), channel_id=1, source_target_pairs={{0,32},{32,64},{64,96},{96,0},{1,33},{33,65},{65,97},{97,1},{2,34}... | collective-permute-start | bytes 393224 | tf_op jit(solution)/shard_map/ppermute | solution.py:120
  133.9 12.2 %collective-permute-start.46 = (f32[64,512]{1,0:T(8,128)S(1)}, f32[64,512]{1,0:T(8,128)S(1)}, u32[]{:S(2)}, u32[]{:S(2)}) collective-permute-start(f32[64,512]{1,0:T(8,128)S(1)} %slice.53), channel_id=1, source_target_pairs={{0,96},{32,0},{64,32},{96,64},{1,97},{33,1},{65,33},{97,65},{2,98}... | collective-permute-start | bytes 393224 | tf_op jit(solution)/shard_map/ppermute | solution.py:120
  163.1 12.4 %collective-permute-start.52 = (f32[128,512]{1,0:T(8,128)}, f32[128,512]{1,0:T(8,128)S(1)}, u32[]{:S(2)}, u32[]{:S(2)}) collective-permute-start(f32[128,512]{1,0:T(8,128)} %get-tuple-element.64), channel_id=1, source_target_pairs={{0,4},{4,8},{8,12},{12,0},{1,5},{5,9},{9,13},{13,1},{2,6},{6,10},{... | collective-permute-start | bytes 786440 | tf_op jit(solution)/shard_map/ppermute | solution.py:120
  173.1 10.9 %collective-permute-start.49 = (f32[128,512]{1,0:T(8,128)}, f32[128,512]{1,0:T(8,128)S(1)}, u32[]{:S(2)}, u32[]{:S(2)}) collective-permute-start(f32[128,512]{1,0:T(8,128)} %get-tuple-element.61), channel_id=1, source_target_pairs={{0,12},{4,0},{8,4},{12,8},{1,13},{5,1},{9,5},{13,9},{2,14},{6,2},{... | collective-permute-start | bytes 786440 | tf_op jit(solution)/shard_map/ppermute | solution.py:120
  187.4 13.3 %collective-permute-start.57 = (f32[128,512]{1,0:T(8,128)S(1)}, f32[128,512]{1,0:T(8,128)S(1)}, u32[]{:S(2)}, u32[]{:S(2)}) collective-permute-start(f32[128,512]{1,0:T(8,128)S(1)} %multiply_select_fusion), channel_id=1, source_target_pairs={{0,64},{1,65},{2,80},{3,81},{4,96},{5,97},{6,112},{7,113},{8,0},{9... | collective-permute-start | bytes 786440 | tf_op jit(solution)/shard_map/ppermute | solution.py:172
  202.2 10.9 %collective-permute-start.60 = (f32[128,512]{1,0:T(8,128)S(1)}, f32[128,512]{1,0:T(8,128)S(1)}, u32[]{:S(2)}, u32[]{:S(2)}) collective-permute-start(f32[128,512]{1,0:T(8,128)S(1)} %collective-permute-done.57), channel_id=1, source_target_pairs={{0,16},{16,0},{1,17},{17,1},{2,18},{18,2},{3,19},{19,3},{4,20},{20... | collective-permute-start | bytes 786440 | tf_op jit(solution)/shard_map/ppermute | solution.py:124
  204.6 9.7 %collective-permute-start.58 = (f32[128,512]{1,0:T(8,128)S(1)}, f32[128,512]{1,0:T(8,128)S(1)}, u32[]{:S(2)}, u32[]{:S(2)}) collective-permute-start(f32[128,512]{1,0:T(8,128)S(1)} %collective-permute-done.57), channel_id=1, source_target_pairs={{0,32},{32,64},{64,96},{96,0},{1,33},{33,65},{65,97},{97,1},{2,34}... | collective-permute-start | bytes 786440 | tf_op jit(solution)/shard_map/ppermute | solution.py:120
  209.6 15.8 %collective-permute-start.62 = (f32[128,512]{1,0:T(8,128)S(1)}, f32[128,512]{1,0:T(8,128)S(1)}, u32[]{:S(2)}, u32[]{:S(2)}) collective-permute-start(f32[128,512]{1,0:T(8,128)S(1)} %collective-permute-done.59), channel_id=1, source_target_pairs={{0,96},{32,0},{64,32},{96,64},{1,97},{33,1},{65,33},{97,65},{2,98}... | collective-permute-start | bytes 786440 | tf_op jit(solution)/shard_map/ppermute | solution.py:120
  210.3 11.8 %collective-permute-start.63 = (f32[128,512]{1,0:T(8,128)S(1)}, f32[128,512]{1,0:T(8,128)S(1)}, u32[]{:S(2)}, u32[]{:S(2)}) collective-permute-start(f32[128,512]{1,0:T(8,128)S(1)} %collective-permute-done.59), channel_id=1, source_target_pairs={{0,16},{16,0},{1,17},{17,1},{2,18},{18,2},{3,19},{19,3},{4,20},{20... | collective-permute-start | bytes 786440 | tf_op jit(solution)/shard_map/ppermute | solution.py:124
  (66 other events, 586.2 us)

commit v3 on v2

--- a/solution.py
+++ b/solution.py
@@ -145,7 +145,8 @@
 def scatter_sum(blk, axes):
     far = blk(2, 1)
     n = far.shape[0] // 2
-    u, w = ring(far[:n], axes, -1), ring(far[n:], axes, 1)
+    u = ring(far[:n], axes, -1)
+    w = ring(far[n:], axes, 1)
     held = lax.optimization_barrier({d: blk(*d) for d in REL[1:]})
     sp, tm = ring(held[2, 0], axes, 1), ring(held[3, 0], axes, -1)
     none = jnp.zeros_like(u)
@@ -221,9 +222,14 @@
     got = flip(give, "core")
     kept = product_part(me, matrix, blocks[4:], dists[4:], partial, 0)
 
+    ready = [kept, got]
+
     def held(da, db):
         j = at(GRID, da, db) * BLK
-        return lax.dynamic_slice_in_dim(kept, j, BLK, 0) + lax.dynamic_slice_in_dim(got, j, BLK, 0)
+        made = lax.dynamic_slice_in_dim(ready[0], j, BLK, 0) + lax.dynamic_slice_in_dim(ready[1], j, BLK, 0)
+        if (da, db) == REL[0]:
+            made, *ready[:] = lax.optimization_barrier((made, *ready))
+        return made
 
     total = scatter_sum(held, GRID)
     block = jnp.where(keep_rows[:, None], 0.5 * (diag + total), F32(0.0))

time: 230 us -> 232 us (level)
  starting transfers between devices: 73.3 us -> 76.9 us
  waiting for transfers between devices: 100 us -> 97.3 us
    ppermute x36, starting transfers between devices: 53.4 us -> 57.6 us  [ring(): return lax.ppermute(v, axes[0], [(i, (i + by) % 4) for i in range(4)])]
    ppermute x1, waiting for transfers between devices: 12.5 us -> 9 us  [turn(): return lax.ppermute(v, ALL, perm)]
  transfers between devices with their start and end apart: 66 -> 66, of which waited for: 36 -> 36; matrix products, arithmetic and copies ran while one was open for 4% -> 5% of each run, Pallas kernels for 6% -> 6%
where the time goes in v3:
time: 232 us; the launch traced here: 231 us
  waiting for transfers between devices  97.3 us (42%)
  starting transfers between devices  76.9 us (33%)
  Pallas kernels  33.1 us (14%)
  other arithmetic  13.5 us (6%)
  local copies, waits for them, and re-layouts  6.66 us (3%)
    ppermute x36, waiting for transfers between devices, ring(): return lax.ppermute(v, axes[0], [(i, (i + by) % 4) for i in range(4)])  63.1 us
    ppermute x36, starting transfers between devices, ring(): return lax.ppermute(v, axes[0], [(i, (i + by) % 4) for i in range(4)])  57.6 us
    ppermute x29, waiting for transfers between devices, flip(): return lax.ppermute(v, axis, [(0, 1), (1, 0)])  25.2 us
    pallas_call x3, Pallas kernels, product_part(): pl.pallas_call(functools.partial(product_kernel, n, int(prev is not None)...  19.7 us
    ppermute x29, starting transfers between devices, flip(): return lax.ppermute(v, axis, [(0, 1), (1, 0)])  18.8 us
    pallas_call x1, Pallas kernels, gram(): pl.pallas_call(functools.partial(gram_kernel, dists, pair), out_shape=tup...  13.4 us
    ppermute x1, waiting for transfers between devices, turn(): return lax.ppermute(v, ALL, perm)  9 us
    select_n x2, other arithmetic, per_device(): jnp.where(owner // 2 == chip, jnp.where(owner % 2 == core, kept, got), F3...  4.65 us
  transfers between devices with their start and end apart: 66, of which 36 were waited for; matrix products, arithmetic and copies ran while one was open for 5% of the time, Pallas kernels for 6%

profile of v3, /device:TPU:0, one launch (start us, length us, event | category | flops | bytes accessed | tf_op | source)
XLA Modules:
  0.0 230.5 jit_solution(878998398291019719)
XLA Ops:
  27.3 3.3 %collective-permute-done.7 = f32[128,512]{1,0:T(8,128)S(1)} collective-permute-done((f32[128,512]{1,0:T(8,128)S(1)}, f32[128,512]{1,0:T(8,128)S(1)}, u32[]{:S(2)}, u32[]{:S(2)}) %collective-permute-start.7) | collective-permute-done | bytes 262176 | tf_op jit(solution)/shard_map/ppermute | solution.py:120
  34.8 4.5 %collective-permute-start.19 = (f32[128,512]{1,0:T(8,128)S(1)}, f32[128,512]{1,0:T(8,128)S(1)}, u32[]{:S(2)}, u32[]{:S(2)}) collective-permute-start(f32[128,512]{1,0:T(8,128)S(1)} %fusion.refs_2_), channel_id=1, source_target_pairs={{0,12},{4,0},{8,4},{12,8},{1,13},{5,1},{9,5},{13,9},{2,14},{6,2},{... | collective-permute-start | bytes 786440 | tf_op jit(solution)/shard_map/ppermute | solution.py:120
  45.2 7.5 %collective-permute-done.23.refs_10_ = f32[128,512]{1,0:T(8,128)S(1)} collective-permute-done((f32[128,512]{1,0:T(8,128)S(1)}, f32[128,512]{1,0:T(8,128)S(1)}, u32[]{:S(2)}, u32[]{:S(2)}) %collective-permute-start.23) | collective-permute-done | bytes 262176 | tf_op jit(solution)/shard_map/ppermute | solution.py:120
  52.9 3.1 %collective-permute-start.25 = (f32[128,512]{1,0:T(8,128)S(1)}, f32[128,512]{1,0:T(8,128)S(1)}, u32[]{:S(2)}, u32[]{:S(2)}) collective-permute-start(f32[128,512]{1,0:T(8,128)S(1)} %collective-permute-done.19.refs_6_), channel_id=1, source_target_pairs={{0,12},{4,0},{8,4},{12,8},{1,13},{5,1},{9,5},{13,9},{2,14},{6,2},{... | collective-permute-start | bytes 786440 | tf_op jit(solution)/shard_map/ppermute | solution.py:120
  59.8 5.3 %collective-permute-done.30 = f32[64,512]{1,0:T(8,128)S(1)} collective-permute-done((f32[64,512]{1,0:T(8,128)S(1)}, f32[64,512]{1,0:T(8,128)S(1)}, u32[]{:S(2)}, u32[]{:S(2)}) %collective-permute-start.30) | collective-permute-done | bytes 131104 | tf_op jit(solution)/shard_map/ppermute | solution.py:120
  69.1 13.4 %shard_map.46 = (f32[128,512]{1,0:T(8,128)}, f32[128,512]{1,0:T(8,128)}, f32[128,512]{1,0:T(8,128)}, f32[128,512]{1,0:T(8,128)}, f32[128,512]{1,0:T(8,128)}, /*i...) custom-call(s32[5]{0:T(128)} %stack.23.me, f32[2048,1024]{1,0:T(8,128)} %refs_3_.5, f32[2048,1024]{1,0:T(8,128)} %refs_3_.5, ...), custom_call_target="tpu_custom_call" | custom-call | tf_op jit(solution)/shard_map/pallas_call | solution.py:67
  92.1 3.5 %collective-permute-start.34 = (f32[128,512]{1,0:T(8,128)S(1)}, f32[128,512]{1,0:T(8,128)S(1)}, u32[]{:S(2)}, u32[]{:S(2)}) collective-permute-start(f32[128,512]{1,0:T(8,128)S(1)} %pad_add_fusion.3), channel_id=1, source_target_pairs={{0,16},{16,0},{1,17},{17,1},{2,18},{18,2},{3,19},{19,3},{4,20},{20... | collective-permute-start | bytes 786440 | tf_op jit(solution)/shard_map/ppermute | solution.py:124
  102.4 3.4 %collective-permute-done.38 = f32[128,512]{1,0:T(8,128)S(1)} collective-permute-done((f32[128,512]{1,0:T(8,128)S(1)}, f32[128,512]{1,0:T(8,128)S(1)}, u32[]{:S(2)}, u32[]{:S(2)}) %collective-permute-start.38) | collective-permute-done | bytes 262176 | tf_op jit(solution)/shard_map/ppermute | solution.py:120
  109.8 5.4 %collective-permute-done.39 = f32[128,512]{1,0:T(8,128)S(1)} collective-permute-done((f32[128,512]{1,0:T(8,128)S(1)}, f32[128,512]{1,0:T(8,128)S(1)}, u32[]{:S(2)}, u32[]{:S(2)}) %collective-permute-start.39) | collective-permute-done | bytes 262176 | tf_op jit(solution)/shard_map/ppermute | solution.py:124
  118.2 7.6 %collective-permute-done.40.refs_7_ = f32[128,512]{1,0:T(8,128)S(1)} collective-permute-done((f32[128,512]{1,0:T(8,128)S(1)}, f32[128,512]{1,0:T(8,128)S(1)}, u32[]{:S(2)}, u32[]{:S(2)}) %collective-permute-start.40) | collective-permute-done | bytes 262176 | tf_op jit(solution)/shard_map/ppermute | solution.py:124
  128.1 3.7 %collective-permute-start.43 = (f32[128,512]{1,0:T(8,128)S(1)}, f32[128,512]{1,0:T(8,128)S(1)}, u32[]{:S(2)}, u32[]{:S(2)}) collective-permute-start(f32[128,512]{1,0:T(8,128)S(1)} %collective-permute-done.42.refs_6_), channel_id=1, source_target_pairs={{0,96},{32,0},{64,32},{96,64},{1,97},{33,1},{65,33},{97,65},{2,98}... | collective-permute-start | bytes 786440 | tf_op jit(solution)/shard_map/ppermute | solution.py:120
  133.8 3.2 %collective-permute-start.46 = (f32[64,512]{1,0:T(8,128)S(1)}, f32[64,512]{1,0:T(8,128)S(1)}, u32[]{:S(2)}, u32[]{:S(2)}) collective-permute-start(f32[64,512]{1,0:T(8,128)S(1)} %slice.53), channel_id=1, source_target_pairs={{0,96},{32,0},{64,32},{96,64},{1,97},{33,1},{65,33},{97,65},{2,98}... | collective-permute-start | bytes 393224 | tf_op jit(solution)/shard_map/ppermute | solution.py:120
  137.8 8.2 %shard_map.47.refs_8_ = f32[2048,512]{1,0:T(8,128)} custom-call(s32[5]{0:T(128)} %stack.23.me, f32[2048,1024]{1,0:T(8,128)} %refs_3_.5, f32[2048,1024]{1,0:T(8,128)} %refs_3_.5, f32[2048,1024]{1,0:T(8,128)} %refs_3_.5, f32[2048,1024]{1,0:T(8,128)} %refs_3_.5, f32[128,512]{1,0:T(8,128)} %copy-done.7, f32[128,512]{1,0:T(8,128)} %copy-done.21, ...), custom_call_target="tpu_custom_call" | custom-call | flops 3221225472 | bytes 8388608 | tf_op jit(solution)/shard_map/pallas_call | solution.py:103
  147.5 5.8 %shard_map.49 = f32[1024,512]{1,0:T(8,128)} custom-call(s32[5]{0:T(128)} %stack.23.me, f32[2048,1024]{1,0:T(8,128)} %refs_3_.5, f32[2048,1024]{1,0:T(8,128)} %refs_3_.5, f32[2048,1024]{1,0:T(8,128)} %refs_3_.5, f32[2048,1024]{1,0:T(8,128)} %refs_3_.5, f32[128,512]{1,0:T(8,128)} %copy-done.2, f32[128,512]{1,0:T(8,128)} %copy-done.5, f32[128,512]{1,0:T(8,128)} %copy-done.3, ...), custom_call_target="tpu_custom_call" | custom-call | flops 1610612736 | bytes 4194304 | tf_op jit(solution)/shard_map/pallas_call | solution.py:103
  153.3 5.8 %shard_map.48 = f32[1024,512]{1,0:T(8,128)} custom-call(s32[5]{0:T(128)} %stack.23.me, f32[2048,1024]{1,0:T(8,128)} %refs_3_.5, f32[2048,1024]{1,0:T(8,128)} %refs_3_.5, f32[2048,1024]{1,0:T(8,128)} %refs_3_.5, f32[2048,1024]{1,0:T(8,128)} %refs_3_.5, f32[128,512]{1,0:T(8,128)} %copy-done.2, f32[128,512]{1,0:T(8,128)} %copy-done.5, f32[128,512]{1,0:T(8,128)} %copy-done.3, ...), custom_call_target="tpu_custom_call" | custom-call | flops 1610612736 | bytes 4194304 | tf_op jit(solution)/shard_map/pallas_call | solution.py:103
  168.3 3.4 %collective-permute-done.54 = f32[64,512]{1,0:T(8,128)S(1)} collective-permute-done((f32[64,512]{1,0:T(8,128)S(1)}, f32[64,512]{1,0:T(8,128)S(1)}, u32[]{:S(2)}, u32[]{:S(2)}) %collective-permute-start.54) | collective-permute-done | bytes 131104 | tf_op jit(solution)/shard_map/ppermute | solution.py:120
  177.4 3.5 %collective-permute-done.55 = f32[128,512]{1,0:T(8,128)S(1)} collective-permute-done((f32[128,512]{1,0:T(8,128)S(1)}, f32[128,512]{1,0:T(8,128)S(1)}, u32[]{:S(2)}, u32[]{:S(2)}) %collective-permute-start.55) | collective-permute-done | bytes 262176 | tf_op jit(solution)/shard_map/ppermute | solution.py:120
  181.8 3.2 %collective-permute-done.49 = f32[128,512]{1,0:T(8,128)S(1)} collective-permute-done((f32[128,512]{1,0:T(8,128)}, f32[128,512]{1,0:T(8,128)S(1)}, u32[]{:S(2)}, u32[]{:S(2)}) %collective-permute-start.49) | collective-permute-done | bytes 262176 | tf_op jit(solution)/shard_map/ppermute | solution.py:120
  188.2 9.0 %collective-permute-done.57 = f32[128,512]{1,0:T(8,128)S(1)} collective-permute-done((f32[128,512]{1,0:T(8,128)S(1)}, f32[128,512]{1,0:T(8,128)S(1)}, u32[]{:S(2)}, u32[]{:S(2)}) %collective-permute-start.57) | collective-permute-done | bytes 262176 | tf_op jit(solution)/shard_map/ppermute | solution.py:173
  197.2 5.6 %collective-permute-start.59 = (f32[128,512]{1,0:T(8,128)S(1)}, f32[128,512]{1,0:T(8,128)S(1)}, u32[]{:S(2)}, u32[]{:S(2)}) collective-permute-start(f32[128,512]{1,0:T(8,128)S(1)} %collective-permute-done.57), channel_id=1, source_target_pairs={{0,96},{32,0},{64,32},{96,64},{1,97},{33,1},{65,33},{97,65},{2,98}... | collective-permute-start | bytes 786440 | tf_op jit(solution)/shard_map/ppermute | solution.py:120
  209.0 3.7 %collective-permute-start.62 = (f32[128,512]{1,0:T(8,128)S(1)}, f32[128,512]{1,0:T(8,128)S(1)}, u32[]{:S(2)}, u32[]{:S(2)}) collective-permute-start(f32[128,512]{1,0:T(8,128)S(1)} %collective-permute-done.59), channel_id=1, source_target_pairs={{0,96},{32,0},{64,32},{96,64},{1,97},{33,1},{65,33},{97,65},{2,98}... | collective-permute-start | bytes 786440 | tf_op jit(solution)/shard_map/ppermute | solution.py:120
  212.7 3.3 %collective-permute-start.63 = (f32[128,512]{1,0:T(8,128)S(1)}, f32[128,512]{1,0:T(8,128)S(1)}, u32[]{:S(2)}, u32[]{:S(2)}) collective-permute-start(f32[128,512]{1,0:T(8,128)S(1)} %collective-permute-done.59), channel_id=1, source_target_pairs={{0,16},{16,0},{1,17},{17,1},{2,18},{18,2},{3,19},{19,3},{4,20},{20... | collective-permute-start | bytes 786440 | tf_op jit(solution)/shard_map/ppermute | solution.py:124
  216.1 7.5 %collective-permute-done.61 = f32[128,512]{1,0:T(8,128)S(1)} collective-permute-done((f32[128,512]{1,0:T(8,128)S(1)}, f32[128,512]{1,0:T(8,128)S(1)}, u32[]{:S(2)}, u32[]{:S(2)}) %collective-permute-start.61) | collective-permute-done | bytes 262176 | tf_op jit(solution)/shard_map/ppermute | solution.py:120
  223.7 3.3 %collective-permute-start.65 = (f32[64,512]{1,0:T(8,128)S(1)}, f32[64,512]{1,0:T(8,128)S(1)}, u32[]{:S(2)}, u32[]{:S(2)}) collective-permute-start(f32[64,512]{1,0:T(8,128)S(1)} %slice.55), channel_id=1, source_target_pairs={{0,96},{32,0},{64,32},{96,64},{1,97},{33,1},{65,33},{97,65},{2,98}... | collective-permute-start | bytes 393224 | tf_op jit(solution)/shard_map/ppermute | solution.py:120
  (208 shorter events, 102.2 us)
Async XLA Ops:
  17.3 9.7 %collective-permute-start.14 = (f32[128,512]{1,0:T(8,128)S(1)}, f32[128,512]{1,0:T(8,128)S(1)}, u32[]{:S(2)}, u32[]{:S(2)}) collective-permute-start(f32[128,512]{1,0:T(8,128)S(1)} %pad_add_fusion.4), channel_id=1, source_target_pairs={{0,12},{4,0},{8,4},{12,8},{1,13},{5,1},{9,5},{13,9},{2,14},{6,2},{... | collective-permute-start | bytes 786440 | tf_op jit(solution)/shard_map/ppermute | solution.py:120
  20.3 10.2 %collective-permute-start.7 = (f32[128,512]{1,0:T(8,128)S(1)}, f32[128,512]{1,0:T(8,128)S(1)}, u32[]{:S(2)}, u32[]{:S(2)}) collective-permute-start(f32[128,512]{1,0:T(8,128)S(1)} %get-tuple-element.41), channel_id=1, source_target_pairs={{0,12},{4,0},{8,4},{12,8},{1,13},{5,1},{9,5},{13,9},{2,14},{6,2},{... | collective-permute-start | bytes 786440 | tf_op jit(solution)/shard_map/ppermute | solution.py:120
  34.8 10.4 %collective-permute-start.19 = (f32[128,512]{1,0:T(8,128)S(1)}, f32[128,512]{1,0:T(8,128)S(1)}, u32[]{:S(2)}, u32[]{:S(2)}) collective-permute-start(f32[128,512]{1,0:T(8,128)S(1)} %fusion.refs_2_), channel_id=1, source_target_pairs={{0,12},{4,0},{8,4},{12,8},{1,13},{5,1},{9,5},{13,9},{2,14},{6,2},{... | collective-permute-start | bytes 786440 | tf_op jit(solution)/shard_map/ppermute | solution.py:120
  40.7 12.0 %collective-permute-start.23 = (f32[128,512]{1,0:T(8,128)S(1)}, f32[128,512]{1,0:T(8,128)S(1)}, u32[]{:S(2)}, u32[]{:S(2)}) collective-permute-start(f32[128,512]{1,0:T(8,128)S(1)} %collective-permute-done.21.refs_8_), channel_id=1, source_target_pairs={{0,4},{4,8},{8,12},{12,0},{1,5},{5,9},{9,13},{13,1},{2,6},{6,10},{... | collective-permute-start | bytes 786440 | tf_op jit(solution)/shard_map/ppermute | solution.py:120
  42.8 13.2 %collective-permute-start.17 = (f32[128,512]{1,0:T(8,128)S(1)}, f32[128,512]{1,0:T(8,128)S(1)}, u32[]{:S(2)}, u32[]{:S(2)}) collective-permute-start(f32[128,512]{1,0:T(8,128)S(1)} %fusion.refs_2_), channel_id=1, source_target_pairs={{0,4},{4,8},{8,12},{12,0},{1,5},{5,9},{9,13},{13,1},{2,6},{6,10},{... | collective-permute-start | bytes 786440 | tf_op jit(solution)/shard_map/ppermute | solution.py:120
  45.2 11.1 %collective-permute-start.27 = (f32[128,512]{1,0:T(8,128)S(1)}, f32[128,512]{1,0:T(8,128)S(1)}, u32[]{:S(2)}, u32[]{:S(2)}) collective-permute-start(f32[128,512]{1,0:T(8,128)S(1)} %collective-permute-done.19.refs_6_), channel_id=1, source_target_pairs={{0,2},{2,0},{1,3},{3,1},{4,6},{6,4},{5,7},{7,5},{8,10},{10,8},{9,1... | collective-permute-start | bytes 786440 | tf_op jit(solution)/shard_map/ppermute | solution.py:124
  52.8 12.3 %collective-permute-start.16 = (f32[128,512]{1,0:T(8,128)S(1)}, f32[128,512]{1,0:T(8,128)S(1)}, u32[]{:S(2)}, u32[]{:S(2)}) collective-permute-start(f32[128,512]{1,0:T(8,128)S(1)} %fusion.refs_2_), channel_id=1, source_target_pairs={{0,1},{1,0},{2,3},{3,2},{4,5},{5,4},{6,7},{7,6},{8,9},{9,8},{10,11... | collective-permute-start | bytes 786440 | tf_op jit(solution)/shard_map/ppermute | solution.py:124
  52.9 12.8 %collective-permute-start.25 = (f32[128,512]{1,0:T(8,128)S(1)}, f32[128,512]{1,0:T(8,128)S(1)}, u32[]{:S(2)}, u32[]{:S(2)}) collective-permute-start(f32[128,512]{1,0:T(8,128)S(1)} %collective-permute-done.19.refs_6_), channel_id=1, source_target_pairs={{0,12},{4,0},{8,4},{12,8},{1,13},{5,1},{9,5},{13,9},{2,14},{6,2},{... | collective-permute-start | bytes 786440 | tf_op jit(solution)/shard_map/ppermute | solution.py:120
  56.1 9.8 %collective-permute-start.18 = (f32[128,512]{1,0:T(8,128)S(1)}, f32[128,512]{1,0:T(8,128)S(1)}, u32[]{:S(2)}, u32[]{:S(2)}) collective-permute-start(f32[128,512]{1,0:T(8,128)S(1)} %collective-permute-done.17.refs_4_), channel_id=1, source_target_pairs={{0,1},{1,0},{2,3},{3,2},{4,5},{5,4},{6,7},{7,6},{8,9},{9,8},{10,11... | collective-permute-start | bytes 786440 | tf_op jit(solution)/shard_map/ppermute | solution.py:124
  56.3 10.0 %collective-permute-start.20 = (f32[128,512]{1,0:T(8,128)S(1)}, f32[128,512]{1,0:T(8,128)S(1)}, u32[]{:S(2)}, u32[]{:S(2)}) collective-permute-start(f32[128,512]{1,0:T(8,128)S(1)} %collective-permute-done.19.refs_6_), channel_id=1, source_target_pairs={{0,1},{1,0},{2,3},{3,2},{4,5},{5,4},{6,7},{7,6},{8,9},{9,8},{10,11... | collective-permute-start | bytes 786440 | tf_op jit(solution)/shard_map/ppermute | solution.py:124
  85.1 14.0 %collective-permute-start.35 = (f32[128,512]{1,0:T(8,128)}, f32[128,512]{1,0:T(8,128)S(1)}, u32[]{:S(2)}, u32[]{:S(2)}) collective-permute-start(f32[128,512]{1,0:T(8,128)} %get-tuple-element.60), channel_id=1, source_target_pairs={{0,32},{32,64},{64,96},{96,0},{1,33},{33,65},{65,97},{97,1},{2,34}... | collective-permute-start | bytes 786440 | tf_op jit(solution)/shard_map/ppermute | solution.py:120
  98.2 10.9 %collective-permute-start.32 = (f32[128,512]{1,0:T(8,128)}, f32[128,512]{1,0:T(8,128)S(1)}, u32[]{:S(2)}, u32[]{:S(2)}) collective-permute-start(f32[128,512]{1,0:T(8,128)} %get-tuple-element.56), channel_id=1, source_target_pairs={{0,96},{32,0},{64,32},{96,64},{1,97},{33,1},{65,33},{97,65},{2,98}... | collective-permute-start | bytes 786440 | tf_op jit(solution)/shard_map/ppermute | solution.py:120
  115.3 10.5 %collective-permute-start.40 = (f32[128,512]{1,0:T(8,128)S(1)}, f32[128,512]{1,0:T(8,128)S(1)}, u32[]{:S(2)}, u32[]{:S(2)}) collective-permute-start(f32[128,512]{1,0:T(8,128)S(1)} %bitcast_add_fusion.refs_4_), channel_id=1, source_target_pairs={{0,16},{16,0},{1,17},{17,1},{2,18},{18,2},{3,19},{19,3},{4,20},{20... | collective-permute-start | bytes 786440 | tf_op jit(solution)/shard_map/ppermute | solution.py:124
  115.4 10.5 %collective-permute-start.42 = (f32[128,512]{1,0:T(8,128)S(1)}, f32[128,512]{1,0:T(8,128)S(1)}, u32[]{:S(2)}, u32[]{:S(2)}) collective-permute-start(f32[128,512]{1,0:T(8,128)S(1)} %bitcast_add_fusion.refs_4_), channel_id=1, source_target_pairs={{0,96},{32,0},{64,32},{96,64},{1,97},{33,1},{65,33},{97,65},{2,98}... | collective-permute-start | bytes 786440 | tf_op jit(solution)/shard_map/ppermute | solution.py:120
  128.1 18.0 %collective-permute-start.43 = (f32[128,512]{1,0:T(8,128)S(1)}, f32[128,512]{1,0:T(8,128)S(1)}, u32[]{:S(2)}, u32[]{:S(2)}) collective-permute-start(f32[128,512]{1,0:T(8,128)S(1)} %collective-permute-done.42.refs_6_), channel_id=1, source_target_pairs={{0,96},{32,0},{64,32},{96,64},{1,97},{33,1},{65,33},{97,65},{2,98}... | collective-permute-start | bytes 786440 | tf_op jit(solution)/shard_map/ppermute | solution.py:120
  133.4 12.6 %collective-permute-start.45 = (f32[64,512]{1,0:T(8,128)S(1)}, f32[64,512]{1,0:T(8,128)S(1)}, u32[]{:S(2)}, u32[]{:S(2)}) collective-permute-start(f32[64,512]{1,0:T(8,128)S(1)} %slice.52), channel_id=1, source_target_pairs={{0,32},{32,64},{64,96},{96,0},{1,33},{33,65},{65,97},{97,1},{2,34}... | collective-permute-start | bytes 393224 | tf_op jit(solution)/shard_map/ppermute | solution.py:120
  133.8 12.2 %collective-permute-start.46 = (f32[64,512]{1,0:T(8,128)S(1)}, f32[64,512]{1,0:T(8,128)S(1)}, u32[]{:S(2)}, u32[]{:S(2)}) collective-permute-start(f32[64,512]{1,0:T(8,128)S(1)} %slice.53), channel_id=1, source_target_pairs={{0,96},{32,0},{64,32},{96,64},{1,97},{33,1},{65,33},{97,65},{2,98}... | collective-permute-start | bytes 393224 | tf_op jit(solution)/shard_map/ppermute | solution.py:120
  163.7 10.8 %collective-permute-start.52 = (f32[128,512]{1,0:T(8,128)}, f32[128,512]{1,0:T(8,128)S(1)}, u32[]{:S(2)}, u32[]{:S(2)}) collective-permute-start(f32[128,512]{1,0:T(8,128)} %get-tuple-element.70), channel_id=1, source_target_pairs={{0,4},{4,8},{8,12},{12,0},{1,5},{5,9},{9,13},{13,1},{2,6},{6,10},{... | collective-permute-start | bytes 786440 | tf_op jit(solution)/shard_map/ppermute | solution.py:120
  174.0 11.0 %collective-permute-start.49 = (f32[128,512]{1,0:T(8,128)}, f32[128,512]{1,0:T(8,128)S(1)}, u32[]{:S(2)}, u32[]{:S(2)}) collective-permute-start(f32[128,512]{1,0:T(8,128)} %get-tuple-element.66), channel_id=1, source_target_pairs={{0,12},{4,0},{8,4},{12,8},{1,13},{5,1},{9,5},{13,9},{2,14},{6,2},{... | collective-permute-start | bytes 786440 | tf_op jit(solution)/shard_map/ppermute | solution.py:120
  197.2 11.8 %collective-permute-start.59 = (f32[128,512]{1,0:T(8,128)S(1)}, f32[128,512]{1,0:T(8,128)S(1)}, u32[]{:S(2)}, u32[]{:S(2)}) collective-permute-start(f32[128,512]{1,0:T(8,128)S(1)} %collective-permute-done.57), channel_id=1, source_target_pairs={{0,96},{32,0},{64,32},{96,64},{1,97},{33,1},{65,33},{97,65},{2,98}... | collective-permute-start | bytes 786440 | tf_op jit(solution)/shard_map/ppermute | solution.py:120
  202.8 13.2 %collective-permute-start.60 = (f32[128,512]{1,0:T(8,128)S(1)}, f32[128,512]{1,0:T(8,128)S(1)}, u32[]{:S(2)}, u32[]{:S(2)}) collective-permute-start(f32[128,512]{1,0:T(8,128)S(1)} %collective-permute-done.57), channel_id=1, source_target_pairs={{0,16},{16,0},{1,17},{17,1},{2,18},{18,2},{3,19},{19,3},{4,20},{20... | collective-permute-start | bytes 786440 | tf_op jit(solution)/shard_map/ppermute | solution.py:124
  205.6 10.3 %collective-permute-start.58 = (f32[128,512]{1,0:T(8,128)S(1)}, f32[128,512]{1,0:T(8,128)S(1)}, u32[]{:S(2)}, u32[]{:S(2)}) collective-permute-start(f32[128,512]{1,0:T(8,128)S(1)} %collective-permute-done.57), channel_id=1, source_target_pairs={{0,32},{32,64},{64,96},{96,0},{1,33},{33,65},{65,97},{97,1},{2,34}... | collective-permute-start | bytes 786440 | tf_op jit(solution)/shard_map/ppermute | solution.py:120
  209.0 18.0 %collective-permute-start.62 = (f32[128,512]{1,0:T(8,128)S(1)}, f32[128,512]{1,0:T(8,128)S(1)}, u32[]{:S(2)}, u32[]{:S(2)}) collective-permute-start(f32[128,512]{1,0:T(8,128)S(1)} %collective-permute-done.59), channel_id=1, source_target_pairs={{0,96},{32,0},{64,32},{96,64},{1,97},{33,1},{65,33},{97,65},{2,98}... | collective-permute-start | bytes 786440 | tf_op jit(solution)/shard_map/ppermute | solution.py:120
  212.7 11.0 %collective-permute-start.63 = (f32[128,512]{1,0:T(8,128)S(1)}, f32[128,512]{1,0:T(8,128)S(1)}, u32[]{:S(2)}, u32[]{:S(2)}) collective-permute-start(f32[128,512]{1,0:T(8,128)S(1)} %collective-permute-done.59), channel_id=1, source_target_pairs={{0,16},{16,0},{1,17},{17,1},{2,18},{18,2},{3,19},{19,3},{4,20},{20... | collective-permute-start | bytes 786440 | tf_op jit(solution)/shard_map/ppermute | solution.py:124
  (66 other events, 583.5 us)

commit v4 on v3

--- a/solution.py
+++ b/solution.py
@@ -194,15 +194,17 @@
     keep_rows = (rows_global < order // 2) == (rows_global < split_index[0])
     diag = (rows_global[:, None] == start + jnp.arange(width, dtype=jnp.int32)[None, :]).astype(F32)
 
-    raw, shift = {}, offset
+    raw, shift, later = {}, offset, offset
     for da, db in REL:
         j = at(GRID, da, db)
         give = lax.dynamic_slice(matrix, ((1 - core) * half + j * BLK, shift), (BLK, width))
         if not raw:
             give, shift = lax.optimization_barrier((give, offset))
         got = flip(give, "core")
-        kept = lax.dynamic_slice(matrix, (core * half + j * BLK, offset if not raw else shift), (BLK, width))
+        kept = lax.dynamic_slice(matrix, (core * half + j * BLK, later), (BLK, width))
         raw[da, db] = jnp.where(owner // 2 == chip, jnp.where(owner % 2 == core, kept, got), F32(0.0))
+        if (da, db) == REL[0]:
+            raw[da, db], later = lax.optimization_barrier((raw[da, db], offset))
     block = scatter_sum(lambda da, db: raw[da, db], GRID)
     block = lax.dot_general(
         block, factor_inverse, (((1,), (1,)), ((), ())), precision=lax.Precision.HIGH, preferred_element_type=F32

time: 232 us -> 234 us (level)
  waiting for transfers between devices: 97.3 us -> 101 us
  starting transfers between devices: 76.9 us -> 74.3 us
    ppermute x29, waiting for transfers between devices: 25.2 us -> 27.9 us  [flip(): return lax.ppermute(v, axis, [(0, 1), (1, 0)])]
  transfers between devices with their start and end apart: 66 -> 66, of which waited for: 36 -> 36; matrix products, arithmetic and copies ran while one was open for 5% -> 4% of each run, Pallas kernels for 6% -> 6%
where the time goes in v4:
time: 234 us; the launch traced here: 233 us
  waiting for transfers between devices  101 us (43%)
  starting transfers between devices  74.3 us (32%)
  Pallas kernels  33.2 us (14%)
  other arithmetic  15.1 us (6%)
  local copies, waits for them, and re-layouts  6.82 us (3%)
    ppermute x36, waiting for transfers between devices, ring(): return lax.ppermute(v, axes[0], [(i, (i + by) % 4) for i in range(4)])  64.7 us
    ppermute x36, starting transfers between devices, ring(): return lax.ppermute(v, axes[0], [(i, (i + by) % 4) for i in range(4)])  56.1 us
    ppermute x29, waiting for transfers between devices, flip(): return lax.ppermute(v, axis, [(0, 1), (1, 0)])  27.9 us
    pallas_call x3, Pallas kernels, product_part(): pl.pallas_call(functools.partial(product_kernel, n, int(prev is not None)...  19.7 us
    ppermute x29, starting transfers between devices, flip(): return lax.ppermute(v, axis, [(0, 1), (1, 0)])  17.1 us
    pallas_call x1, Pallas kernels, gram(): pl.pallas_call(functools.partial(gram_kernel, dists, pair), out_shape=tup...  13.4 us
    ppermute x1, waiting for transfers between devices, turn(): return lax.ppermute(v, ALL, perm)  8.43 us
    select_n x2, other arithmetic, per_device(): jnp.where(owner // 2 == chip, jnp.where(owner % 2 == core, kept, got), F3...  5.05 us
  transfers between devices with their start and end apart: 66, of which 36 were waited for; matrix products, arithmetic and copies ran while one was open for 4% of the time, Pallas kernels for 6%

profile of v4, /device:TPU:0, one launch (start us, length us, event | category | flops | bytes accessed | tf_op | source)
XLA Modules:
  0.0 233.3 jit_solution(7229213771554654578)
XLA Ops:
  6.2 3.1 %select_select_fusion = (f32[128,512]{1,0:T(8,128)S(1)}, f32[128,512]{1,0:T(8,128)S(1)}, f32[128,512]{1,0:T(8,128)}, f32[128,512]{1,0:T(8,128)}, f32[128,512]{1,...) fusion(f32[128,512]{1,0:T(8,128)S(1)} %collective-permute-done.7, f32[2048,1024]{1,0:T(8,128)} %refs_3_.5, ...), kind=kLoop, calls=%fused_computation.24 | loop fusion | flops 131072 | bytes 3932198 | tf_op jit(solution)/shard_map/jit(_where)/select_n | solution.py:205
  30.6 3.4 %collective-permute-done.8 = f32[128,512]{1,0:T(8,128)S(1)} collective-permute-done((f32[128,512]{1,0:T(8,128)S(1)}, f32[128,512]{1,0:T(8,128)S(1)}, u32[]{:S(2)}, u32[]{:S(2)}) %collective-permute-start.8) | collective-permute-done | bytes 262176 | tf_op jit(solution)/shard_map/ppermute | solution.py:120
  38.4 4.0 %collective-permute-start.19 = (f32[128,512]{1,0:T(8,128)S(1)}, f32[128,512]{1,0:T(8,128)S(1)}, u32[]{:S(2)}, u32[]{:S(2)}) collective-permute-start(f32[128,512]{1,0:T(8,128)S(1)} %fusion.refs_2_), channel_id=1, source_target_pairs={{0,12},{4,0},{8,4},{12,8},{1,13},{5,1},{9,5},{13,9},{2,14},{6,2},{... | collective-permute-start | bytes 786440 | tf_op jit(solution)/shard_map/ppermute | solution.py:120
  48.3 7.2 %collective-permute-done.23.refs_10_ = f32[128,512]{1,0:T(8,128)S(1)} collective-permute-done((f32[128,512]{1,0:T(8,128)S(1)}, f32[128,512]{1,0:T(8,128)S(1)}, u32[]{:S(2)}, u32[]{:S(2)}) %collective-permute-start.23) | collective-permute-done | bytes 262176 | tf_op jit(solution)/shard_map/ppermute | solution.py:120
  55.7 3.1 %collective-permute-start.25 = (f32[128,512]{1,0:T(8,128)S(1)}, f32[128,512]{1,0:T(8,128)S(1)}, u32[]{:S(2)}, u32[]{:S(2)}) collective-permute-start(f32[128,512]{1,0:T(8,128)S(1)} %collective-permute-done.19.refs_6_), channel_id=1, source_target_pairs={{0,12},{4,0},{8,4},{12,8},{1,13},{5,1},{9,5},{13,9},{2,14},{6,2},{... | collective-permute-start | bytes 786440 | tf_op jit(solution)/shard_map/ppermute | solution.py:120
  62.5 5.3 %collective-permute-done.30 = f32[64,512]{1,0:T(8,128)S(1)} collective-permute-done((f32[64,512]{1,0:T(8,128)S(1)}, f32[64,512]{1,0:T(8,128)S(1)}, u32[]{:S(2)}, u32[]{:S(2)}) %collective-permute-start.30) | collective-permute-done | bytes 131104 | tf_op jit(solution)/shard_map/ppermute | solution.py:120
  71.9 13.4 %shard_map.46 = (f32[128,512]{1,0:T(8,128)}, f32[128,512]{1,0:T(8,128)}, f32[128,512]{1,0:T(8,128)}, f32[128,512]{1,0:T(8,128)}, f32[128,512]{1,0:T(8,128)}, /*i...) custom-call(s32[5]{0:T(128)} %stack.23.me, f32[2048,1024]{1,0:T(8,128)} %refs_3_.5, f32[2048,1024]{1,0:T(8,128)} %refs_3_.5, ...), custom_call_target="tpu_custom_call" | custom-call | tf_op jit(solution)/shard_map/pallas_call | solution.py:67
  95.0 3.8 %collective-permute-start.34 = (f32[128,512]{1,0:T(8,128)S(1)}, f32[128,512]{1,0:T(8,128)S(1)}, u32[]{:S(2)}, u32[]{:S(2)}) collective-permute-start(f32[128,512]{1,0:T(8,128)S(1)} %pad_add_fusion.3), channel_id=1, source_target_pairs={{0,16},{16,0},{1,17},{17,1},{2,18},{18,2},{3,19},{19,3},{4,20},{20... | collective-permute-start | bytes 786440 | tf_op jit(solution)/shard_map/ppermute | solution.py:124
  105.3 3.8 %collective-permute-done.38 = f32[128,512]{1,0:T(8,128)S(1)} collective-permute-done((f32[128,512]{1,0:T(8,128)S(1)}, f32[128,512]{1,0:T(8,128)S(1)}, u32[]{:S(2)}, u32[]{:S(2)}) %collective-permute-start.38) | collective-permute-done | bytes 262176 | tf_op jit(solution)/shard_map/ppermute | solution.py:120
  112.6 6.5 %collective-permute-done.39 = f32[128,512]{1,0:T(8,128)S(1)} collective-permute-done((f32[128,512]{1,0:T(8,128)S(1)}, f32[128,512]{1,0:T(8,128)S(1)}, u32[]{:S(2)}, u32[]{:S(2)}) %collective-permute-start.39) | collective-permute-done | bytes 262176 | tf_op jit(solution)/shard_map/ppermute | solution.py:124
  122.0 7.5 %collective-permute-done.40.refs_7_ = f32[128,512]{1,0:T(8,128)S(1)} collective-permute-done((f32[128,512]{1,0:T(8,128)S(1)}, f32[128,512]{1,0:T(8,128)S(1)}, u32[]{:S(2)}, u32[]{:S(2)}) %collective-permute-start.40) | collective-permute-done | bytes 262176 | tf_op jit(solution)/shard_map/ppermute | solution.py:124
  131.7 3.7 %collective-permute-start.43 = (f32[128,512]{1,0:T(8,128)S(1)}, f32[128,512]{1,0:T(8,128)S(1)}, u32[]{:S(2)}, u32[]{:S(2)}) collective-permute-start(f32[128,512]{1,0:T(8,128)S(1)} %collective-permute-done.42.refs_6_), channel_id=1, source_target_pairs={{0,96},{32,0},{64,32},{96,64},{1,97},{33,1},{65,33},{97,65},{2,98}... | collective-permute-start | bytes 786440 | tf_op jit(solution)/shard_map/ppermute | solution.py:120
  137.5 3.2 %collective-permute-start.46 = (f32[64,512]{1,0:T(8,128)S(1)}, f32[64,512]{1,0:T(8,128)S(1)}, u32[]{:S(2)}, u32[]{:S(2)}) collective-permute-start(f32[64,512]{1,0:T(8,128)S(1)} %slice.51), channel_id=1, source_target_pairs={{0,96},{32,0},{64,32},{96,64},{1,97},{33,1},{65,33},{97,65},{2,98}... | collective-permute-start | bytes 393224 | tf_op jit(solution)/shard_map/ppermute | solution.py:120
  141.5 8.2 %shard_map.47.refs_8_ = f32[2048,512]{1,0:T(8,128)} custom-call(s32[5]{0:T(128)} %stack.23.me, f32[2048,1024]{1,0:T(8,128)} %refs_3_.5, f32[2048,1024]{1,0:T(8,128)} %refs_3_.5, f32[2048,1024]{1,0:T(8,128)} %refs_3_.5, f32[2048,1024]{1,0:T(8,128)} %refs_3_.5, f32[128,512]{1,0:T(8,128)} %copy-done.7, f32[128,512]{1,0:T(8,128)} %copy-done.21, ...), custom_call_target="tpu_custom_call" | custom-call | flops 3221225472 | bytes 8388608 | tf_op jit(solution)/shard_map/pallas_call | solution.py:103
  151.1 5.8 %shard_map.49 = f32[1024,512]{1,0:T(8,128)} custom-call(s32[5]{0:T(128)} %stack.23.me, f32[2048,1024]{1,0:T(8,128)} %refs_3_.5, f32[2048,1024]{1,0:T(8,128)} %refs_3_.5, f32[2048,1024]{1,0:T(8,128)} %refs_3_.5, f32[2048,1024]{1,0:T(8,128)} %refs_3_.5, f32[128,512]{1,0:T(8,128)} %copy-done.2, f32[128,512]{1,0:T(8,128)} %copy-done.5, f32[128,512]{1,0:T(8,128)} %copy-done.3, ...), custom_call_target="tpu_custom_call" | custom-call | flops 1610612736 | bytes 4194304 | tf_op jit(solution)/shard_map/pallas_call | solution.py:103
  157.0 5.8 %shard_map.48 = f32[1024,512]{1,0:T(8,128)} custom-call(s32[5]{0:T(128)} %stack.23.me, f32[2048,1024]{1,0:T(8,128)} %refs_3_.5, f32[2048,1024]{1,0:T(8,128)} %refs_3_.5, f32[2048,1024]{1,0:T(8,128)} %refs_3_.5, f32[2048,1024]{1,0:T(8,128)} %refs_3_.5, f32[128,512]{1,0:T(8,128)} %copy-done.2, f32[128,512]{1,0:T(8,128)} %copy-done.5, f32[128,512]{1,0:T(8,128)} %copy-done.3, ...), custom_call_target="tpu_custom_call" | custom-call | flops 1610612736 | bytes 4194304 | tf_op jit(solution)/shard_map/pallas_call | solution.py:103
  171.7 3.4 %collective-permute-done.54 = f32[64,512]{1,0:T(8,128)S(1)} collective-permute-done((f32[64,512]{1,0:T(8,128)S(1)}, f32[64,512]{1,0:T(8,128)S(1)}, u32[]{:S(2)}, u32[]{:S(2)}) %collective-permute-start.54) | collective-permute-done | bytes 131104 | tf_op jit(solution)/shard_map/ppermute | solution.py:120
  180.9 3.5 %collective-permute-done.55 = f32[128,512]{1,0:T(8,128)S(1)} collective-permute-done((f32[128,512]{1,0:T(8,128)S(1)}, f32[128,512]{1,0:T(8,128)S(1)}, u32[]{:S(2)}, u32[]{:S(2)}) %collective-permute-start.55) | collective-permute-done | bytes 262176 | tf_op jit(solution)/shard_map/ppermute | solution.py:120
  185.2 3.1 %collective-permute-done.49 = f32[128,512]{1,0:T(8,128)S(1)} collective-permute-done((f32[128,512]{1,0:T(8,128)}, f32[128,512]{1,0:T(8,128)S(1)}, u32[]{:S(2)}, u32[]{:S(2)}) %collective-permute-start.49) | collective-permute-done | bytes 262176 | tf_op jit(solution)/shard_map/ppermute | solution.py:120
  192.2 8.4 %collective-permute-done.57 = f32[128,512]{1,0:T(8,128)S(1)} collective-permute-done((f32[128,512]{1,0:T(8,128)S(1)}, f32[128,512]{1,0:T(8,128)S(1)}, u32[]{:S(2)}, u32[]{:S(2)}) %collective-permute-start.57) | collective-permute-done | bytes 262176 | tf_op jit(solution)/shard_map/ppermute | solution.py:173
  200.7 5.8 %collective-permute-start.59 = (f32[128,512]{1,0:T(8,128)S(1)}, f32[128,512]{1,0:T(8,128)S(1)}, u32[]{:S(2)}, u32[]{:S(2)}) collective-permute-start(f32[128,512]{1,0:T(8,128)S(1)} %collective-permute-done.57), channel_id=1, source_target_pairs={{0,96},{32,0},{64,32},{96,64},{1,97},{33,1},{65,33},{97,65},{2,98}... | collective-permute-start | bytes 786440 | tf_op jit(solution)/shard_map/ppermute | solution.py:120
  211.7 3.7 %collective-permute-start.62 = (f32[128,512]{1,0:T(8,128)S(1)}, f32[128,512]{1,0:T(8,128)S(1)}, u32[]{:S(2)}, u32[]{:S(2)}) collective-permute-start(f32[128,512]{1,0:T(8,128)S(1)} %collective-permute-done.59), channel_id=1, source_target_pairs={{0,96},{32,0},{64,32},{96,64},{1,97},{33,1},{65,33},{97,65},{2,98}... | collective-permute-start | bytes 786440 | tf_op jit(solution)/shard_map/ppermute | solution.py:120
  218.0 8.3 %collective-permute-done.61 = f32[128,512]{1,0:T(8,128)S(1)} collective-permute-done((f32[128,512]{1,0:T(8,128)S(1)}, f32[128,512]{1,0:T(8,128)S(1)}, u32[]{:S(2)}, u32[]{:S(2)}) %collective-permute-start.61) | collective-permute-done | bytes 262176 | tf_op jit(solution)/shard_map/ppermute | solution.py:120
  226.5 3.3 %collective-permute-start.65 = (f32[64,512]{1,0:T(8,128)S(1)}, f32[64,512]{1,0:T(8,128)S(1)}, u32[]{:S(2)}, u32[]{:S(2)}) collective-permute-start(f32[64,512]{1,0:T(8,128)S(1)} %slice.53), channel_id=1, source_target_pairs={{0,96},{32,0},{64,32},{96,64},{1,97},{33,1},{65,33},{97,65},{2,98}... | collective-permute-start | bytes 393224 | tf_op jit(solution)/shard_map/ppermute | solution.py:120
  (209 shorter events, 103.7 us)
Async XLA Ops:
  20.7 9.7 %collective-permute-start.14 = (f32[128,512]{1,0:T(8,128)S(1)}, f32[128,512]{1,0:T(8,128)S(1)}, u32[]{:S(2)}, u32[]{:S(2)}) collective-permute-start(f32[128,512]{1,0:T(8,128)S(1)} %pad_add_fusion.4), channel_id=1, source_target_pairs={{0,12},{4,0},{8,4},{12,8},{1,13},{5,1},{9,5},{13,9},{2,14},{6,2},{... | collective-permute-start | bytes 786440 | tf_op jit(solution)/shard_map/ppermute | solution.py:120
  23.7 10.3 %collective-permute-start.8 = (f32[128,512]{1,0:T(8,128)S(1)}, f32[128,512]{1,0:T(8,128)S(1)}, u32[]{:S(2)}, u32[]{:S(2)}) collective-permute-start(f32[128,512]{1,0:T(8,128)S(1)} %get-tuple-element.45), channel_id=1, source_target_pairs={{0,12},{4,0},{8,4},{12,8},{1,13},{5,1},{9,5},{13,9},{2,14},{6,2},{... | collective-permute-start | bytes 786440 | tf_op jit(solution)/shard_map/ppermute | solution.py:120
  44.4 11.1 %collective-permute-start.23 = (f32[128,512]{1,0:T(8,128)S(1)}, f32[128,512]{1,0:T(8,128)S(1)}, u32[]{:S(2)}, u32[]{:S(2)}) collective-permute-start(f32[128,512]{1,0:T(8,128)S(1)} %collective-permute-done.21.refs_8_), channel_id=1, source_target_pairs={{0,4},{4,8},{8,12},{12,0},{1,5},{5,9},{9,13},{13,1},{2,6},{6,10},{... | collective-permute-start | bytes 786440 | tf_op jit(solution)/shard_map/ppermute | solution.py:120
  45.9 12.9 %collective-permute-start.17 = (f32[128,512]{1,0:T(8,128)S(1)}, f32[128,512]{1,0:T(8,128)S(1)}, u32[]{:S(2)}, u32[]{:S(2)}) collective-permute-start(f32[128,512]{1,0:T(8,128)S(1)} %fusion.refs_2_), channel_id=1, source_target_pairs={{0,4},{4,8},{8,12},{12,0},{1,5},{5,9},{9,13},{13,1},{2,6},{6,10},{... | collective-permute-start | bytes 786440 | tf_op jit(solution)/shard_map/ppermute | solution.py:120
  47.8 11.2 %collective-permute-start.27 = (f32[128,512]{1,0:T(8,128)S(1)}, f32[128,512]{1,0:T(8,128)S(1)}, u32[]{:S(2)}, u32[]{:S(2)}) collective-permute-start(f32[128,512]{1,0:T(8,128)S(1)} %collective-permute-done.19.refs_6_), channel_id=1, source_target_pairs={{0,2},{2,0},{1,3},{3,1},{4,6},{6,4},{5,7},{7,5},{8,10},{10,8},{9,1... | collective-permute-start | bytes 786440 | tf_op jit(solution)/shard_map/ppermute | solution.py:124
  55.6 12.3 %collective-permute-start.16 = (f32[128,512]{1,0:T(8,128)S(1)}, f32[128,512]{1,0:T(8,128)S(1)}, u32[]{:S(2)}, u32[]{:S(2)}) collective-permute-start(f32[128,512]{1,0:T(8,128)S(1)} %fusion.refs_2_), channel_id=1, source_target_pairs={{0,1},{1,0},{2,3},{3,2},{4,5},{5,4},{6,7},{7,6},{8,9},{9,8},{10,11... | collective-permute-start | bytes 786440 | tf_op jit(solution)/shard_map/ppermute | solution.py:124
  55.7 12.8 %collective-permute-start.25 = (f32[128,512]{1,0:T(8,128)S(1)}, f32[128,512]{1,0:T(8,128)S(1)}, u32[]{:S(2)}, u32[]{:S(2)}) collective-permute-start(f32[128,512]{1,0:T(8,128)S(1)} %collective-permute-done.19.refs_6_), channel_id=1, source_target_pairs={{0,12},{4,0},{8,4},{12,8},{1,13},{5,1},{9,5},{13,9},{2,14},{6,2},{... | collective-permute-start | bytes 786440 | tf_op jit(solution)/shard_map/ppermute | solution.py:120
  58.8 10.0 %collective-permute-start.18 = (f32[128,512]{1,0:T(8,128)S(1)}, f32[128,512]{1,0:T(8,128)S(1)}, u32[]{:S(2)}, u32[]{:S(2)}) collective-permute-start(f32[128,512]{1,0:T(8,128)S(1)} %collective-permute-done.17.refs_4_), channel_id=1, source_target_pairs={{0,1},{1,0},{2,3},{3,2},{4,5},{5,4},{6,7},{7,6},{8,9},{9,8},{10,11... | collective-permute-start | bytes 786440 | tf_op jit(solution)/shard_map/ppermute | solution.py:124
  59.0 10.0 %collective-permute-start.20 = (f32[128,512]{1,0:T(8,128)S(1)}, f32[128,512]{1,0:T(8,128)S(1)}, u32[]{:S(2)}, u32[]{:S(2)}) collective-permute-start(f32[128,512]{1,0:T(8,128)S(1)} %collective-permute-done.19.refs_6_), channel_id=1, source_target_pairs={{0,1},{1,0},{2,3},{3,2},{4,5},{5,4},{6,7},{7,6},{8,9},{9,8},{10,11... | collective-permute-start | bytes 786440 | tf_op jit(solution)/shard_map/ppermute | solution.py:124
  87.9 14.3 %collective-permute-start.35 = (f32[128,512]{1,0:T(8,128)}, f32[128,512]{1,0:T(8,128)S(1)}, u32[]{:S(2)}, u32[]{:S(2)}) collective-permute-start(f32[128,512]{1,0:T(8,128)} %get-tuple-element.64), channel_id=1, source_target_pairs={{0,32},{32,64},{64,96},{96,0},{1,33},{33,65},{65,97},{97,1},{2,34}... | collective-permute-start | bytes 786440 | tf_op jit(solution)/shard_map/ppermute | solution.py:120
  101.4 10.6 %collective-permute-start.32 = (f32[128,512]{1,0:T(8,128)}, f32[128,512]{1,0:T(8,128)S(1)}, u32[]{:S(2)}, u32[]{:S(2)}) collective-permute-start(f32[128,512]{1,0:T(8,128)} %get-tuple-element.60), channel_id=1, source_target_pairs={{0,96},{32,0},{64,32},{96,64},{1,97},{33,1},{65,33},{97,65},{2,98}... | collective-permute-start | bytes 786440 | tf_op jit(solution)/shard_map/ppermute | solution.py:120
  109.1 10.0 %collective-permute-start.39 = (f32[128,512]{1,0:T(8,128)S(1)}, f32[128,512]{1,0:T(8,128)S(1)}, u32[]{:S(2)}, u32[]{:S(2)}) collective-permute-start(f32[128,512]{1,0:T(8,128)S(1)} %add.722), channel_id=1, source_target_pairs={{0,16},{16,0},{1,17},{17,1},{2,18},{18,2},{3,19},{19,3},{4,20},{20... | collective-permute-start | bytes 786440 | tf_op jit(solution)/shard_map/ppermute | solution.py:124
  119.2 10.3 %collective-permute-start.40 = (f32[128,512]{1,0:T(8,128)S(1)}, f32[128,512]{1,0:T(8,128)S(1)}, u32[]{:S(2)}, u32[]{:S(2)}) collective-permute-start(f32[128,512]{1,0:T(8,128)S(1)} %bitcast_add_fusion.refs_4_), channel_id=1, source_target_pairs={{0,16},{16,0},{1,17},{17,1},{2,18},{18,2},{3,19},{19,3},{4,20},{20... | collective-permute-start | bytes 786440 | tf_op jit(solution)/shard_map/ppermute | solution.py:124
  119.3 10.2 %collective-permute-start.42 = (f32[128,512]{1,0:T(8,128)S(1)}, f32[128,512]{1,0:T(8,128)S(1)}, u32[]{:S(2)}, u32[]{:S(2)}) collective-permute-start(f32[128,512]{1,0:T(8,128)S(1)} %bitcast_add_fusion.refs_4_), channel_id=1, source_target_pairs={{0,96},{32,0},{64,32},{96,64},{1,97},{33,1},{65,33},{97,65},{2,98}... | collective-permute-start | bytes 786440 | tf_op jit(solution)/shard_map/ppermute | solution.py:120
  131.7 18.0 %collective-permute-start.43 = (f32[128,512]{1,0:T(8,128)S(1)}, f32[128,512]{1,0:T(8,128)S(1)}, u32[]{:S(2)}, u32[]{:S(2)}) collective-permute-start(f32[128,512]{1,0:T(8,128)S(1)} %collective-permute-done.42.refs_6_), channel_id=1, source_target_pairs={{0,96},{32,0},{64,32},{96,64},{1,97},{33,1},{65,33},{97,65},{2,98}... | collective-permute-start | bytes 786440 | tf_op jit(solution)/shard_map/ppermute | solution.py:120
  137.1 12.6 %collective-permute-start.45 = (f32[64,512]{1,0:T(8,128)S(1)}, f32[64,512]{1,0:T(8,128)S(1)}, u32[]{:S(2)}, u32[]{:S(2)}) collective-permute-start(f32[64,512]{1,0:T(8,128)S(1)} %slice.50), channel_id=1, source_target_pairs={{0,32},{32,64},{64,96},{96,0},{1,33},{33,65},{65,97},{97,1},{2,34}... | collective-permute-start | bytes 393224 | tf_op jit(solution)/shard_map/ppermute | solution.py:120
  137.5 12.2 %collective-permute-start.46 = (f32[64,512]{1,0:T(8,128)S(1)}, f32[64,512]{1,0:T(8,128)S(1)}, u32[]{:S(2)}, u32[]{:S(2)}) collective-permute-start(f32[64,512]{1,0:T(8,128)S(1)} %slice.51), channel_id=1, source_target_pairs={{0,96},{32,0},{64,32},{96,64},{1,97},{33,1},{65,33},{97,65},{2,98}... | collective-permute-start | bytes 393224 | tf_op jit(solution)/shard_map/ppermute | solution.py:120
  167.5 10.5 %collective-permute-start.52 = (f32[128,512]{1,0:T(8,128)}, f32[128,512]{1,0:T(8,128)S(1)}, u32[]{:S(2)}, u32[]{:S(2)}) collective-permute-start(f32[128,512]{1,0:T(8,128)} %get-tuple-element.74), channel_id=1, source_target_pairs={{0,4},{4,8},{8,12},{12,0},{1,5},{5,9},{9,13},{13,1},{2,6},{6,10},{... | collective-permute-start | bytes 786440 | tf_op jit(solution)/shard_map/ppermute | solution.py:120
  177.4 10.9 %collective-permute-start.49 = (f32[128,512]{1,0:T(8,128)}, f32[128,512]{1,0:T(8,128)S(1)}, u32[]{:S(2)}, u32[]{:S(2)}) collective-permute-start(f32[128,512]{1,0:T(8,128)} %get-tuple-element.70), channel_id=1, source_target_pairs={{0,12},{4,0},{8,4},{12,8},{1,13},{5,1},{9,5},{13,9},{2,14},{6,2},{... | collective-permute-start | bytes 786440 | tf_op jit(solution)/shard_map/ppermute | solution.py:120
  191.0 9.6 %collective-permute-start.57 = (f32[128,512]{1,0:T(8,128)S(1)}, f32[128,512]{1,0:T(8,128)S(1)}, u32[]{:S(2)}, u32[]{:S(2)}) collective-permute-start(f32[128,512]{1,0:T(8,128)S(1)} %multiply_select_fusion), channel_id=1, source_target_pairs={{0,64},{1,65},{2,80},{3,81},{4,96},{5,97},{6,112},{7,113},{8,0},{9... | collective-permute-start | bytes 786440 | tf_op jit(solution)/shard_map/ppermute | solution.py:173
  200.7 11.0 %collective-permute-start.59 = (f32[128,512]{1,0:T(8,128)S(1)}, f32[128,512]{1,0:T(8,128)S(1)}, u32[]{:S(2)}, u32[]{:S(2)}) collective-permute-start(f32[128,512]{1,0:T(8,128)S(1)} %collective-permute-done.57), channel_id=1, source_target_pairs={{0,96},{32,0},{64,32},{96,64},{1,97},{33,1},{65,33},{97,65},{2,98}... | collective-permute-start | bytes 786440 | tf_op jit(solution)/shard_map/ppermute | solution.py:120
  206.5 10.9 %collective-permute-start.60 = (f32[128,512]{1,0:T(8,128)S(1)}, f32[128,512]{1,0:T(8,128)S(1)}, u32[]{:S(2)}, u32[]{:S(2)}) collective-permute-start(f32[128,512]{1,0:T(8,128)S(1)} %collective-permute-done.57), channel_id=1, source_target_pairs={{0,16},{16,0},{1,17},{17,1},{2,18},{18,2},{3,19},{19,3},{4,20},{20... | collective-permute-start | bytes 786440 | tf_op jit(solution)/shard_map/ppermute | solution.py:124
  211.7 18.1 %collective-permute-start.62 = (f32[128,512]{1,0:T(8,128)S(1)}, f32[128,512]{1,0:T(8,128)S(1)}, u32[]{:S(2)}, u32[]{:S(2)}) collective-permute-start(f32[128,512]{1,0:T(8,128)S(1)} %collective-permute-done.59), channel_id=1, source_target_pairs={{0,96},{32,0},{64,32},{96,64},{1,97},{33,1},{65,33},{97,65},{2,98}... | collective-permute-start | bytes 786440 | tf_op jit(solution)/shard_map/ppermute | solution.py:120
  215.4 11.1 %collective-permute-start.63 = (f32[128,512]{1,0:T(8,128)S(1)}, f32[128,512]{1,0:T(8,128)S(1)}, u32[]{:S(2)}, u32[]{:S(2)}) collective-permute-start(f32[128,512]{1,0:T(8,128)S(1)} %collective-permute-done.59), channel_id=1, source_target_pairs={{0,16},{16,0},{1,17},{17,1},{2,18},{18,2},{3,19},{19,3},{4,20},{20... | collective-permute-start | bytes 786440 | tf_op jit(solution)/shard_map/ppermute | solution.py:124
  (66 other events, 588.8 us)
